TPU v7x, 128 devices: a whole 4x4x4 slice. The times are simulated.
128 devices in a mesh: row: 8 (over x_lo, z), col: 16 (over y, x_hi, core).
Axes of the slice: x: 4 (x_hi: 2, x_lo: 2; x = x_hi * 2 + x_lo), y: 4, z: 4, core: 2. Of those that a mesh axis runs over, the one named last changes fastest.
Arguments:
- amplitudes: bfloat16 [32, 32, 12, 4096], P('row', 'col'), may hold values from -6 to 6
- integrals: bfloat16 [32, 32, 47, 4096], P('row', 'col'), may hold values from -0.125 to 0.125
- pair_lists: int32 [8, 12, 2], replicated, may hold values from 0 to 46, as said below
- tile_counts: int32 [8], replicated, may hold values from 1 to 12, as said below
Outputs:
- symmetric: float32 [32, 32, 12, 4096], P('row', 'col')
Inputs may be any that keep to these rules, and one draw needn't show every extreme that they name: `pair_lists`: each grid row lists 12 distinct ordered pairs of different tiles. `tile_counts`: the largest count equals 12.
All inputs are finite; a program needn't handle non-finite values.
Results may differ from a plain program's by a relative error of at most 0.0029.
Values may be sent and summed in bfloat16 or wider, within the bound.
A program may use at most 128 MiB of HBM per device.

v0:
```python
import jax
import jax.numpy as jnp
from jax import lax
from jax.sharding import PartitionSpec as P

TILE = 64


def spread(block, axis, owner):
    block = jnp.where(lax.axis_index(axis) == owner, block, jnp.zeros_like(block))
    return lax.psum(block, axis)


def on_device(amplitudes, integrals, pair_lists, tile_counts):
    occ_row, occ_col, slot_count, square = amplitudes.shape
    tile_width = TILE
    row_devices = lax.axis_size("row")
    col_devices = lax.axis_size("col")
    col_ratio = col_devices // row_devices
    my_row = lax.axis_index("row")
    my_col = lax.axis_index("col")
    partner_row = my_col // col_ratio
    tile_first = pair_lists[:, :, 0]
    tile_second = pair_lists[:, :, 1]
    packed = jnp.take(integrals, tile_second.reshape(-1), axis=2)
    packed = packed.reshape(occ_row, occ_col, row_devices, slot_count, square)
    received = lax.all_to_all(packed, "row", split_axis=2, concat_axis=0, tiled=True)
    received = received.reshape(occ_row * row_devices, occ_col, slot_count, square)
    piece = lax.all_gather(amplitudes, "col", axis=1, tiled=True)
    piece_count = piece.shape[1]
    left_tiles = piece.reshape(occ_row, piece_count, slot_count, tile_width, tile_width)
    right_tiles = received.reshape(piece_count, occ_col, slot_count, tile_width, tile_width)
    cycle_sum = jnp.einsum(
        "iksac,kjscb->ijsab", left_tiles, right_tiles, preferred_element_type=jnp.float32
    )
    my_count = lax.dynamic_index_in_dim(tile_counts, my_row, 0, keepdims=False)
    live_slots = (jnp.arange(slot_count, dtype=jnp.int32) < my_count).astype(jnp.float32)
    cycle_value = (cycle_sum * live_slots[None, None, :, None, None]).astype(jnp.bfloat16)
    cycle = cycle_value.reshape(occ_row, occ_col, slot_count, square)
    residual_strip = lax.all_gather(cycle, "col", axis=1, tiled=True)
    mirror_part = lax.dynamic_slice_in_dim(residual_strip, my_col % col_ratio * occ_col, occ_col, 0)
    mirror_whole = spread(mirror_part, "row", partner_row)
    mirror_block = lax.dynamic_slice_in_dim(mirror_whole, my_row * occ_row, occ_row, 1)
    mirror_block = mirror_block.reshape(occ_col, occ_row, slot_count, tile_width, tile_width)
    mine_first = lax.dynamic_index_in_dim(tile_first, my_row, 0, keepdims=False)
    mine_second = lax.dynamic_index_in_dim(tile_second, my_row, 0, keepdims=False)
    their_first = lax.dynamic_index_in_dim(tile_first, partner_row, 0, keepdims=False)
    their_second = lax.dynamic_index_in_dim(tile_second, partner_row, 0, keepdims=False)
    pair_match = (
        (mine_first[:, None] == their_second[None, :])
        & (mine_second[:, None] == their_first[None, :])
    ).astype(jnp.bfloat16)
    crossed = jnp.einsum(
        "st,jitba->ijsab", pair_match, mirror_block, preferred_element_type=jnp.float32
    )
    own_part = cycle_value.astype(jnp.float32)
    symmetric = (own_part + crossed) * live_slots[None, None, :, None, None]
    return symmetric.reshape(occ_row, occ_col, slot_count, square)


def solution(mesh):
    return jax.shard_map(
        on_device,
        mesh=mesh,
        in_specs=(P("row", "col", None, None), P("row", "col", None, None), P(), P()),
        out_specs=P("row", "col", None, None),
        check_vma=False,
    )
```

profile of v0, /device:TPU:3, one launch (start us, length us, event | category | flops | bytes accessed | tf_op | source)
XLA Modules:
  0.0 505.2 jit_solution(17754718859662884650)
XLA Ops:
  6.5 0.0 copy-start
  6.5 0.0 all-gather.3.cloned.1.call-start
  6.5 2.8 copy.18
  9.3 0.0 all-gather.3.cloned.1.call-update
  9.3 0.8 fusion.29
  10.1 0.1 reshape_squeeze.6
  10.2 0.0 copy-done
  10.2 15.2 %gather_fusion = bf16[96,4,2,4096]{3,2,1,0:T(2,128)(2,1)} fusion(bf16[4,2,47,4096]{3,1,2,0:T(2,128)(2,1)S(1)} %copy-done, s32[1024]{0:T(1024)S(1)} %pad_clamp_fusion), kind=kCustom, calls=%fused_computation | custom fusion | bytes 12583296 | tf_op jit(solution)/shard_map/jit(_take)/gather | solution.py:25
  25.5 8.5 %broadcast_select_fusion.1 = bf16[4,2,8,12,4096]{4,1,3,0,2:T(2,128)(2,1)} fusion(pred[8,12]{1,0:T(8,128)(4,1)S(1)} %compare_and_fusion, bf16[4,2,8,12,4096]{4,1,0,3,2:T(2,128)(2,1)} %bitcast.67), kind=kLoop, calls=%fused_computation.5 | loop fusion | flops 3145728 | bytes 12583008 | tf_op jit(solution)/shard_map/jit(_take)/select_n | solution.py:25
  33.9 0.0 copy-start.3
  33.9 6.3 %all-to-all-start = ((bf16[4,2,8,12,4096]{4,1,3,0,2:T(2,128)(2,1)}), bf16[4,2,8,12,4096]{4,1,3,0,2:T(2,128)(2,1)}, u32[]{:S(2)}, u32[]{:S(2)}) async-start(bf16[4,2,8,12,4096]{4,1,3,0,2:T(2,128)(2,1)} %broadcast_select_fusion.1), calls=%async_computation | async-start | bytes 12582912 | tf_op jit(solution)/shard_map/all_to_all | solution.py:27
  40.3 0.0 all-gather.5.cloned.1.call-start
  40.3 0.0 copy-done.3
  40.3 0.6 dynamic_slice.23
  40.9 0.6 compare_convert_fusion
  41.4 100.4 %all-to-all-done = bf16[4,2,8,12,4096]{4,1,3,0,2:T(2,128)(2,1)} async-done(((bf16[4,2,8,12,4096]{4,1,3,0,2:T(2,128)(2,1)}), bf16[4,2,8,12,4096]{4,1,3,0,2:T(2,128)(2,1)}, u32[]{:S(2)}, u32[]{:S(2)}) %all-to-all-start) | async-done | bytes 6291488 | tf_op jit(solution)/shard_map/all_to_all | solution.py:27
  141.8 20.6 %reshape_reshape.3 = bf16[32,2,12,64,64]{4,3,1,2,0:T(8,128)(2,1)} reshape(bf16[8,4,2,1,12,4096]{5,2,4,1,0,3:T(2,128)(2,1)} %bitcast.5) | data formatting | bytes 12582912 | tf_op jit(solution)/shard_map/reshape;reshape | solution.py:32
  162.4 0.0 all-gather.3.cloned.1.call-done
  162.4 14.4 %copy.19 = bf16[4,32,12,4096]{3,1,0,2:T(8,128)(2,1)} copy(bf16[4,32,12,4096]{3,0,2,1:T(4,128)(2,1)} %all-gather.3.cloned.1.call-done) | data formatting | bytes 25165824 | tf_op jit(solution)/shard_map/all_gather | solution.py:29
  176.9 34.4 %reshape.81 = bf16[4,32,12,64,64,1]{4,3,1,0,2,5:T(8,128)(2,1)} reshape(bf16[4,32,12,4096]{3,1,0,2:T(8,128)(2,1)} %copy.19) | data formatting | bytes 25165824 | tf_op jit(solution)/shard_map/reshape | solution.py:31
  211.2 19.0 %fusion.11 = bf16[4,2,12,64,64]{3,4,0,1,2:T(8,128)(2,1)S(1)} fusion(f32[12]{0:T(128)S(1)} %compare_convert_fusion, bf16[4,32,12,64,64,1]{4,3,1,0,2,5:T(8,128)(2,1)} %reshape.81, bf16[32,2,12,64,64]{4,3,1,2,0:T(8,128)(2,1)} %reshape_reshape.3), kind=kOutput, calls=%fused_computation.12 | convolution fusion | flops 1611399168 | bytes 19660848 | tf_op jit(solution)/shard_map/iksac,kjscb->ijsab/dot_general | solution.py:33
  230.2 0.0 copy-start.2
  230.3 1.8 copy.33
  232.0 3.7 reshape.85
  235.7 0.0 all-gather.5.cloned.1.call-update
  235.7 0.3 all-reduce.2.cloned.1.call-start
  236.0 93.1 %all-gather.5.cloned.1.call-done = bf16[4,32,12,4096]{3,0,2,1:T(4,128)(2,1)} async-done(((bf16[4,2,12,4096]{3,0,2,1:T(4,128)(2,1)}), bf16[4,32,12,4096]{3,0,2,1:T(4,128)(2,1)}) %all-gather.5.cloned.1.call-update) | async-done | bytes 12582928 | tf_op jit(solution)/shard_map/all_gather | solution.py:40
  329.1 10.8 %broadcast_select_fusion = bf16[2,32,12,4096]{3,0,2,1:T(2,128)(2,1)} fusion(pred[]{:T(512)S(6)} %eq.39, bf16[4,32,12,4096]{3,0,2,1:T(4,128)(2,1)} %all-gather.5.cloned.1.call-done, s32[]{:T(128)S(6)} %select_n.65), kind=kLoop, calls=%fused_computation.4 | loop fusion | flops 3145728 | bytes 12582917 | tf_op jit(solution)/shard_map/jit(_where)/select_n | solution.py:10
  339.9 0.0 copy-done.2
  339.9 0.0 all-reduce.2.cloned.1.call-update
  339.9 142.5 %all-reduce.2.cloned.1.call-done = bf16[2,32,12,4096]{3,0,2,1:T(2,128)(2,1)} async-done(((bf16[2,32,12,4096]{3,0,2,1:T(2,128)(2,1)}), bf16[2,32,12,4096]{3,0,2,1:T(2,128)(2,1)}) %all-reduce.2.cloned.1.call-update) | async-done | bytes 6291472 | tf_op jit(solution)/shard_map/psum | solution.py:11
  482.5 2.0 constant_dynamic-slice_fusion.4
  484.5 1.0 reshape.86
  485.5 1.1 fusion.5
  486.6 0.0 copy-start.1
  486.6 4.3 fusion.3
  490.9 3.6 copy.26
  494.5 4.2 reshape.71
  498.7 0.0 copy-done.1
  (5 shorter events, 0.0 us)
Async XLA Ops:
  6.5 3.7 copy-start
  6.5 155.9 %all-gather.3.cloned.1.call-start = ((), (), s32[]{:S(2)}) async-start(), calls=%async_computation.1 | async-start | bytes 13369344 | tf_op jit(solution)/shard_map/all_gather | solution.py:29
  33.9 6.4 %copy-start.3 = (s32[8]{0:T(128)S(1)}, s32[8]{0:T(128)}, u32[]{:S(2)}) copy-start(s32[8]{0:T(128)} %param.7) | copy-start | bytes 100
  33.9 107.9 %all-to-all-start = ((bf16[4,2,8,12,4096]{4,1,3,0,2:T(2,128)(2,1)}), bf16[4,2,8,12,4096]{4,1,3,0,2:T(2,128)(2,1)}, u32[]{:S(2)}, u32[]{:S(2)}) async-start(bf16[4,2,8,12,4096]{4,1,3,0,2:T(2,128)(2,1)} %broadcast_select_fusion.1), calls=%async_computation | async-start | bytes 12582912 | tf_op jit(solution)/shard_map/all_to_all | solution.py:27
  40.3 288.8 %all-gather.5.cloned.1.call-start = ((), (), s32[]{:S(2)}) async-start(), calls=%async_computation.2 | async-start | bytes 13369344 | tf_op jit(solution)/shard_map/all_gather | solution.py:40
  230.2 109.6 %copy-start.2 = (bf16[4,2,12,64,64]{3,4,0,1,2:T(8,128)(2,1)}, bf16[4,2,12,64,64]{3,4,0,1,2:T(8,128)(2,1)S(1)}, u32[]{:S(2)}) copy-start(bf16[4,2,12,64,64]{3,4,0,1,2:T(8,128)(2,1)S(1)} %fusion.11) | copy-start | bytes 2359300
  235.7 246.7 %all-reduce.2.cloned.1.call-start = ((), (), s32[]{:S(2)}) async-start(), calls=%async_computation.3 | async-start | bytes 12582912 | tf_op jit(solution)/shard_map/psum | solution.py:11
  486.6 12.0 %copy-start.1 = (bf16[4,2,47,4096]{3,1,2,0:T(2,128)(2,1)S(1)}, bf16[4,2,47,4096]{3,1,2,0:T(2,128)(2,1)}, u32[]{:S(2)}) copy-start(bf16[4,2,47,4096]{3,1,2,0:T(2,128)(2,1)} %param.5) | copy-start | bytes 9240580
Sparse Core Ops, SparseCore 0:
  9.8 126.5 all-gather.2
  235.8 93.2 all-gather.4
  340.0 142.4 all-reduce.1
where the time goes:
time: 509 us; the launch traced here: 505 us
  waiting for transfers between devices  336 us (66%)
  local copies, waits for them, and re-layouts  105 us (21%)
  other arithmetic  24.1 us (5%)
  matrix products  20.1 us (4%)
  between operations  13.2 us (3%)
  starting transfers between devices  6.61 us (1%)
    psum x1, waiting for transfers between devices, spread(): return lax.psum(block, axis)  143 us
    all_to_all x1, waiting for transfers between devices, on_device(): lax.all_to_all(packed, 'row', split_axis=2, concat_axis=0, tiled=True)  100 us
    all_gather x1, waiting for transfers between devices, on_device(): residual_strip = lax.all_gather(cycle, 'col', axis=1, tiled=True)  93.1 us
    reshape x1, local copies, waits for them, and re-layouts, on_device(): piece.reshape(occ_row, piece_count, slot_count, tile_width, tile_width)  34.4 us
    another operation x1, local copies, waits for them, and re-layouts, on_device(): received.reshape(piece_count, occ_col, slot_count, tile_width, tile_width)  20.6 us
    dot_general x1, matrix products, on_device(): jnp.einsum('iksac,kjscb->ijsab', left_tiles, right_tiles, preferred_eleme...  19 us
    gather x1, local copies, waits for them, and re-layouts, on_device(): packed = jnp.take(integrals, tile_second.reshape(-1), axis=2)  15.2 us
    all_gather x1, local copies, waits for them, and re-layouts, on_device(): piece = lax.all_gather(amplitudes, 'col', axis=1, tiled=True)  14.4 us
  transfers between devices with their start and end apart: 4, of which 3 were waited for; matrix products, arithmetic and copies ran while one was open for 9% of the time, Pallas kernels for 0%

commit v1 on v0

v1 whole, which is shorter than its diff:
```python
import functools

import jax
import jax.numpy as jnp
import numpy as np
from jax import lax
from jax.experimental import pallas as pl
from jax.experimental.pallas import tpu as pltpu
from jax.sharding import PartitionSpec as P

MESH = pl.DeviceIdType.MESH
ROWS = 8
TILE = 64
HALF = TILE // 2
LANES = 128


def merge_matrix(permute):
    out = np.zeros((2 * LANES, 2 * LANES), np.float32)
    for operand in range(2):
        for h in range(2):
            for c in range(TILE):
                place = (c % 2) * HALF + c // 2 if permute else c
                out[operand * LANES + h * TILE + c, h * LANES + operand * TILE + place] = 1.0
    return out


def untangle_matrix():
    out = np.zeros((LANES, LANES), np.float32)
    for j in range(2):
        for h in range(2):
            for p in range(HALF):
                out[j * TILE + h * HALF + p, j * TILE + 2 * p + h] = 1.0
    return out


def pack_left(amp_ref, mat_ref, out_ref):
    occ, _, slots = amp_ref.shape[:3]
    half = slots // 2
    for i in range(occ):
        left = amp_ref[i, 0].reshape(slots * HALF, LANES)
        right = amp_ref[i, 1].reshape(slots * HALF, LANES)
        both = jnp.concatenate([left, right], axis=1)
        made = jnp.dot(both, mat_ref[...], preferred_element_type=jnp.float32).astype(jnp.bfloat16)
        for h in range(2):
            rows = made[:, h * LANES : (h + 1) * LANES].reshape(2, half, HALF, LANES)
            out_ref[:, :, i * TILE + h * HALF : i * TILE + (h + 1) * HALF, :] = rows


def pack_right(list_ref, int_ref, mat_ref, out_ref):
    row = pl.program_id(0)
    occ = int_ref.shape[0]
    half = out_ref.shape[2]
    for s in range(2 * half):
        tile = list_ref[row, s]
        left = int_ref[:, 0, tile].reshape(occ * HALF, LANES)
        right = int_ref[:, 1, tile].reshape(occ * HALF, LANES)
        both = jnp.concatenate([left, right], axis=1)
        made = jnp.dot(both, mat_ref[...], preferred_element_type=jnp.float32).astype(jnp.bfloat16)
        for k in range(occ):
            for g in range(2):
                out_ref[0, s // half, s % half, k * TILE + g * HALF : k * TILE + (g + 1) * HALF, :] = made[
                    k * HALF : (k + 1) * HALF, g * LANES : (g + 1) * LANES
                ]


def exchange(a_ref, w_ref, own_ref, mir_ref, abuf, wbuf, cbuf, a_send, a_recv, f_send, w_send, w_recv, c_send, c_recv, l_sem):
    row = lax.axis_index("row")
    col = lax.axis_index("col")
    core = lax.rem(col, 2)
    other = 1 - core
    chip = col // 2
    xh = lax.rem(chip, 2)
    y = chip // 2
    xl, z = row // 4, lax.rem(row, 4)
    half = abuf.shape[1]
    diagonal = chip == row

    def col_of(y_at, xh_at, core_at):
        return (lax.rem(y_at, 4) * 2 + xh_at) * 2 + core_at

    def row_of(step):
        return lax.rem(xl + step // 4, 2) * 4 + lax.rem(z + step % 4, 4)

    barrier = pltpu.get_barrier_semaphore()

    def greet(row_at, col_at):
        pl.semaphore_signal(barrier, inc=1, device_id={"row": row_at, "col": col_at}, device_id_type=MESH)

    greet(row, chip * 2 + other)
    for step in range(1, ROWS):
        for e in range(2):
            greet(row_of(step), chip * 2 + e)
    for e in range(2):
        greet(row, col_of(y, 1 - xh, e))
        for dy in range(1, 4):
            greet(row, col_of(y + dy, xh, e))

    @pl.when(jnp.logical_not(diagonal))
    def _():
        for e in range(2):
            greet(chip, row * 2 + e)

    pl.semaphore_wait(barrier, jnp.where(diagonal, 23, 25))

    def remote(src, dst, send, recv, row_at, col_at):
        return pltpu.make_async_remote_copy(
            src_ref=src, dst_ref=dst, send_sem=send, recv_sem=recv,
            device_id={"row": row_at, "col": col_at}, device_id_type=MESH,
        )

    started = []

    def go(copy):
        copy.start()
        started.append(copy)

    for e in range(2):
        go(remote(a_ref.at[e], abuf.at[col], a_send.at[0, e], a_recv.at[col], row, col_of(y, 1 - xh, e)))
    for step in (4, 5, 7, 6):
        for e in range(2):
            go(remote(w_ref.at[row_of(step), e], wbuf.at[row, core], w_send.at[step, e], w_recv.at[row, core], row_of(step), chip * 2 + e))
    for step in (1, 3, 2):
        for e in range(2):
            go(remote(w_ref.at[row_of(step), e], wbuf.at[row, core], w_send.at[step, e], w_recv.at[row, core], row_of(step), chip * 2 + e))
    for dy in (1, 3, 2):
        for e in range(2):
            go(remote(a_ref.at[e], abuf.at[col], a_send.at[dy, e], a_recv.at[col], row, col_of(y + dy, xh, e)))
    go(remote(a_ref.at[other], abuf.at[col], a_send.at[4, 0], a_recv.at[col], row, chip * 2 + other))
    go(remote(w_ref.at[row, other], wbuf.at[row, core], w_send.at[0, 0], w_recv.at[row, core], row, chip * 2 + other))
    local_a = pltpu.make_async_copy(a_ref.at[core], abuf.at[col], l_sem.at[0])
    local_w = pltpu.make_async_copy(w_ref.at[row, core], wbuf.at[row, core], l_sem.at[1])
    local_a.start()
    local_w.start()

    def arrived(buf, sem):
        pltpu.make_async_copy(buf, buf, sem).wait()

    for e in range(2):
        at = col_of(y, 1 - xh, e)
        arrived(abuf.at[at], a_recv.at[at])
        for dy in (1, 3, 2):
            go(remote(abuf.at[at], abuf.at[at], f_send.at[e, dy], a_recv.at[at], row, col_of(y + dy, xh, core)))

    local_a.wait()
    local_w.wait()
    mate = chip * 2 + other
    arrived(abuf.at[mate], a_recv.at[mate])
    arrived(wbuf.at[row, other], w_recv.at[row, other])
    for dy in (1, 3, 2):
        for xq in range(2):
            for e in range(2):
                at = col_of(y + dy, xq, e)
                arrived(abuf.at[at], a_recv.at[at])
    for step in range(1, ROWS):
        for e in range(2):
            arrived(wbuf.at[row_of(step), e], w_recv.at[row_of(step), e])

    @pl.loop(0, half)
    def _(s):
        total = jnp.zeros((4 * TILE, 4 * TILE), jnp.float32)
        for r in range(ROWS):
            left = jnp.concatenate([abuf[2 * r, s], abuf[2 * r + 1, s]], axis=1)
            right = jnp.concatenate([wbuf[r, 0, s], wbuf[r, 1, s]], axis=1)
            total = total + jnp.dot(left, right, preferred_element_type=jnp.float32)
        made = total.astype(jnp.bfloat16)
        cbuf[0, s] = made[:, :LANES]
        cbuf[1, s] = made[:, LANES:]

    pair = remote(cbuf.at[other], own_ref.at[core], c_send.at[0], c_recv.at[0], row, mate)
    go(pair)
    keep = pltpu.make_async_copy(cbuf.at[core], own_ref.at[core], l_sem.at[0])
    keep.start()

    @pl.when(jnp.logical_not(diagonal))
    def _():
        for q in range(2):
            remote(
                cbuf.at[:, :, pl.ds(q * LANES, LANES)], mir_ref.at[core], c_send.at[1 + q], c_recv.at[1 + core],
                chip, row * 2 + q,
            ).start()
        for q in range(2):
            arrived(mir_ref.at[q], c_recv.at[1 + q])
        for q in range(2):
            arrived(mir_ref.at[core], c_send.at[1 + q])

    @pl.when(diagonal)
    def _():
        there = remote(
            cbuf.at[:, :, pl.ds(other * LANES, LANES)], mir_ref.at[core], c_send.at[1], c_recv.at[1 + core], row, mate
        )
        there.start()
        here = pltpu.make_async_copy(cbuf.at[:, :, pl.ds(core * LANES, LANES)], mir_ref.at[core], c_send.at[2])
        here.start()
        arrived(mir_ref.at[other], c_recv.at[1 + other])
        there.wait_send()
        here.wait()

    keep.wait()
    arrived(own_ref.at[other], c_recv.at[0])
    for copy in started:
        copy.wait_send()


def finish(live_ref, hit_ref, at_ref, own_ref, mir_ref, mat_ref, out_ref, turn):
    slots = out_ref.shape[2]
    half = slots // 2
    lane = lax.broadcasted_iota(jnp.int32, (HALF, LANES), 1)
    low = lane < TILE

    def fold(even, odd):
        first = jnp.where(low, even, pltpu.roll(odd, TILE, 1))
        second = jnp.where(low, pltpu.roll(even, TILE, 1), odd)
        return first, second

    for s in range(slots):
        live = live_ref[s]
        hit = hit_ref[s]
        t = at_ref[s]
        for jp in range(2):
            block = mir_ref[t // half, jp, lax.rem(t, half)]
            turned = lax.dot_general(block, mat_ref[...], (((0,), (0,)), ((), ())), preferred_element_type=jnp.float32)
            turn[...] = turned * hit
            for u in range(2):
                i = jp * 2 + u
                even = turn[pl.ds(u * TILE, HALF, stride=2), :]
                odd = turn[pl.ds(u * TILE + 1, HALF, stride=2), :]
                top = own_ref[s // half, s % half, i * TILE : i * TILE + HALF, :].astype(jnp.float32)
                bottom = own_ref[s // half, s % half, i * TILE + HALF : (i + 1) * TILE, :].astype(jnp.float32)
                first, second = fold((top + even) * live, (bottom + odd) * live)
                out_ref[i, 0, s] = first
                out_ref[i, 1, s] = second


def on_device(amplitudes, integrals, pair_lists, tile_counts):
    occ_row, occ_col, slots, square = amplitudes.shape
    half = slots // 2
    tiles = integrals.shape[2]
    row = lax.axis_index("row")
    col = lax.axis_index("col")
    partner = col // 2
    bf16 = jnp.bfloat16
    vmem = pl.BlockSpec(memory_space=pltpu.VMEM)
    smem = pl.BlockSpec(memory_space=pltpu.SMEM)
    anywhere = pl.BlockSpec(memory_space=pl.ANY)

    amp = amplitudes.reshape(occ_row, occ_col, slots, HALF, LANES)
    integ = integrals.reshape(occ_row, occ_col, tiles, HALF, LANES)
    a_send = pl.pallas_call(
        pack_left,
        name="pack_left",
        out_shape=jax.ShapeDtypeStruct((2, half, occ_row * TILE, LANES), bf16),
        in_specs=[vmem, vmem],
        out_specs=vmem,
        compiler_params=pltpu.CompilerParams(vmem_limit_bytes=32 << 20),
    )(amp, jnp.asarray(merge_matrix(True), bf16))
    w_send = pl.pallas_call(
        pack_right,
        name="pack_right",
        out_shape=jax.ShapeDtypeStruct((ROWS, 2, half, occ_row * TILE, LANES), bf16),
        grid_spec=pltpu.PrefetchScalarGridSpec(
            num_scalar_prefetch=1,
            grid=(ROWS,),
            in_specs=[
                pl.BlockSpec((occ_row, occ_col, tiles, HALF, LANES), lambda r, lists: (0, 0, 0, 0, 0)),
                pl.BlockSpec((2 * LANES, 2 * LANES), lambda r, lists: (0, 0)),
            ],
            out_specs=pl.BlockSpec((1, 2, half, occ_row * TILE, LANES), lambda r, lists: (r, 0, 0, 0, 0)),
        ),
        compiler_params=pltpu.CompilerParams(vmem_limit_bytes=32 << 20),
    )(pair_lists[:, :, 1], integ, jnp.asarray(merge_matrix(False), bf16))

    own, mirror = pl.pallas_call(
        exchange,
        name="exchange",
        out_shape=(
            jax.ShapeDtypeStruct((2, half, occ_row * TILE, LANES), bf16),
            jax.ShapeDtypeStruct((2, 2, half, LANES, LANES), bf16),
        ),
        in_specs=[anywhere, anywhere],
        out_specs=(anywhere, anywhere),
        scratch_shapes=[
            pltpu.VMEM((16, half, occ_row * TILE, LANES), bf16),
            pltpu.VMEM((ROWS, 2, half, occ_row * TILE, LANES), bf16),
            pltpu.VMEM((2, half, occ_row * TILE, LANES), bf16),
            pltpu.SemaphoreType.DMA((5, 2)),
            pltpu.SemaphoreType.DMA((16,)),
            pltpu.SemaphoreType.DMA((2, 4)),
            pltpu.SemaphoreType.DMA((ROWS, 2)),
            pltpu.SemaphoreType.DMA((ROWS, 2)),
            pltpu.SemaphoreType.DMA((3,)),
            pltpu.SemaphoreType.DMA((3,)),
            pltpu.SemaphoreType.DMA((2,)),
        ],
        compiler_params=pltpu.CompilerParams(collective_id=0, has_side_effects=True, vmem_limit_bytes=40 << 20),
    )(a_send, w_send)

    mine = lax.dynamic_index_in_dim(pair_lists, row, 0, keepdims=False)
    theirs = lax.dynamic_index_in_dim(pair_lists, partner, 0, keepdims=False)
    match = (mine[:, None, 0] == theirs[None, :, 1]) & (mine[:, None, 1] == theirs[None, :, 0])
    their_live = jnp.arange(slots, dtype=jnp.int32) < tile_counts[partner]
    match = match & their_live[None, :]
    hit = jnp.any(match, axis=1).astype(jnp.float32)
    at = jnp.argmax(match, axis=1).astype(jnp.int32)
    live = (jnp.arange(slots, dtype=jnp.int32) < tile_counts[row]).astype(jnp.float32)

    packed = pl.pallas_call(
        finish,
        name="finish",
        out_shape=jax.ShapeDtypeStruct((occ_row, occ_col, slots, HALF, LANES), jnp.float32),
        in_specs=[smem, smem, smem, vmem, vmem, vmem],
        out_specs=vmem,
        scratch_shapes=[pltpu.VMEM((LANES, LANES), jnp.float32)],
        compiler_params=pltpu.CompilerParams(vmem_limit_bytes=32 << 20),
    )(live, hit, at, own, mirror, jnp.asarray(untangle_matrix(), bf16))
    return packed.reshape(occ_row, occ_col, slots, square)


def solution(mesh):
    return jax.shard_map(
        on_device,
        mesh=mesh,
        in_specs=(P("row", "col", None, None), P("row", "col", None, None), P(), P()),
        out_specs=P("row", "col", None, None),
        check_vma=False,
    )
```

time: 509 us -> 186 us (0.37)
  the two profiles are of different devices: /device:TPU:3 before, /device:TPU:7 now
where the time goes in v1:
time: 186 us; the launch traced here: 185 us
  Pallas kernels  165 us (89%)
  local copies, waits for them, and re-layouts  18.4 us (10%)
  other arithmetic  2.24 us (1%)
    pallas_call x1, Pallas kernels, on_device(): pl.pallas_call(exchange, name='exchange', out_shape=(jax.ShapeDtypeStruct...  159 us
    reshape x2, local copies, waits for them, and re-layouts, on_device(): integ = integrals.reshape(occ_row, occ_col, tiles, HALF, LANES)  7.48 us
    unnamed x14, local copies, waits for them, and re-layouts  6.02 us

profile of v1, /device:TPU:7, one launch (start us, length us, event | category | flops | bytes accessed | tf_op | source)
XLA Modules:
  0.0 185.3 jit_solution(9689828433652104750)
XLA Ops:
  0.0 0.7 dynamic-slice_bitcast_fusion.1
  0.7 1.4 fusion.1
  2.1 0.6 iota_compare_fusion
  2.8 0.7 iota_reduce_fusion
  3.5 0.2 fusion
  3.7 0.7 compare_convert_fusion.live_ref
  4.4 6.9 %reshape.18 = bf16[4,2,47,32,128]{4,3,1,2,0:T(8,128)(2,1)S(1)} reshape(bf16[4,2,47,4096]{3,1,2,0:T(2,128)(2,1)} %param.8) | data formatting | bytes 6160384 | tf_op jit(solution)/shard_map/reshape | solution.py:248
  11.3 0.0 copy-start.6
  11.3 0.0 copy-start.2
  11.3 0.6 copy.20.int_ref
  11.9 0.1 copy-done.6
  12.0 0.2 copy-done.2
  12.2 0.0 copy-start.5
  12.2 3.7 %pack_right.1.w_ref = bf16[8,2,6,256,128]{4,3,2,1,0:T(8,128)(2,1)S(1)} custom-call(s32[8,12]{1,0:T(8,128)S(1)} %bitcast.25, bf16[4,2,47,32,128]{4,3,2,1,0:T(8,128)(2,1)S(1)} %copy.20.int_ref, bf16[256,256]{1,0:T(8,128)(2,1)S(1)} %copy-done.2), custom_call_target="tpu_custom_call" | custom-call | tf_op jit(solution)/shard_map/pack_right/pallas_call | solution.py:257
  15.9 0.0 copy-start
  15.9 2.7 %copy-done = bf16[8,2,6,256,128]{4,3,2,1,0:T(8,128)(2,1)} copy-done((bf16[8,2,6,256,128]{4,3,2,1,0:T(8,128)(2,1)}, bf16[8,2,6,256,128]{4,3,2,1,0:T(8,128)(2,1)S(1)}, u32[]{:S(2)}) %copy-start) | copy-done | bytes 6291480
  18.6 0.0 copy-done.5
  18.6 0.0 copy-start.3
  18.6 0.6 reshape.15
  19.2 0.1 copy.16.amp_ref
  19.2 0.2 copy-done.3
  19.5 0.4 pack_left.1.a_ref
  19.9 0.0 copy-start.1
  19.9 2.8 %copy-done.1 = bf16[8,2,6,256,128]{4,3,2,1,0:T(8,128)(2,1)S(1)} copy-done((bf16[8,2,6,256,128]{4,3,2,1,0:T(8,128)(2,1)S(1)}, bf16[8,2,6,256,128]{4,3,2,1,0:T(8,128)(2,1)}, u32[]{:S(2)}) %copy-start.1) | copy-done | bytes 6291480
  22.6 0.0 copy-start.4
  22.6 159.1 %exchange.1 = (bf16[2,6,256,128]{3,2,1,0:T(8,128)(2,1)S(1)}, bf16[2,2,6,128,128]{4,3,2,1,0:T(8,128)(2,1)S(1)}) custom-call(bf16[2,6,256,128]{3,2,1,0:T(8,128)(2,1)S(1)} %pack_left.1.a_ref, bf16[8,2,6,256,128]{4,3,2,1,0:T(8,128)(2,1)S(1)} %copy-done.1), custom_call_target="tpu_custom_call" | custom-call | tf_op jit(solution)/shard_map/exchange/pallas_call | solution.py:273
  181.7 0.0 copy-done.4
  181.7 1.4 finish.1
  183.1 0.2 copy.19
  183.3 2.0 %reshape.17 = f32[4,2,12,4096]{3,1,2,0:T(2,128)} reshape(f32[4,2,12,32,128]{4,3,1,2,0:T(8,128)S(1)} %copy.19) | data formatting | bytes 3145728 | tf_op jit(solution)/shard_map/reshape | solution.py:316
  (3 shorter events, 0.0 us)
Async XLA Ops:
  11.3 0.7 copy-start.6
  11.3 0.9 copy-start.2
  12.2 6.4 %copy-start.5 = (bf16[4,2,12,4096]{3,1,2,0:T(2,128)(2,1)S(1)}, bf16[4,2,12,4096]{3,1,2,0:T(2,128)(2,1)}, u32[]{:S(2)}) copy-start(bf16[4,2,12,4096]{3,1,2,0:T(2,128)(2,1)} %param.7) | copy-start | bytes 2359300
  15.9 2.7 %copy-start = (bf16[8,2,6,256,128]{4,3,2,1,0:T(8,128)(2,1)}, bf16[8,2,6,256,128]{4,3,2,1,0:T(8,128)(2,1)S(1)}, u32[]{:S(2)}) copy-start(bf16[8,2,6,256,128]{4,3,2,1,0:T(8,128)(2,1)S(1)} %pack_right.1.w_ref) | copy-start | bytes 18874372
  18.6 0.9 copy-start.3
  19.9 2.8 %copy-start.1 = (bf16[8,2,6,256,128]{4,3,2,1,0:T(8,128)(2,1)S(1)}, bf16[8,2,6,256,128]{4,3,2,1,0:T(8,128)(2,1)}, u32[]{:S(2)}) copy-start(bf16[8,2,6,256,128]{4,3,2,1,0:T(8,128)(2,1)} %copy-done) | copy-start | bytes 18874372
  22.6 159.1 %copy-start.4 = (bf16[128,128]{1,0:T(8,128)(2,1)S(1)}, bf16[128,128]{1,0:T(8,128)(2,1)}, u32[]{:S(2)}) copy-start(bf16[128,128]{1,0:T(8,128)(2,1)} %constant.46.clone.mat_ref) | copy-start | bytes 98308

commit v2 on v0

v2 whole, which is shorter than its diff:
```python
import functools

import jax
import jax.numpy as jnp
import numpy as np
from jax import lax
from jax.experimental import pallas as pl
from jax.experimental.pallas import tpu as pltpu
from jax.sharding import PartitionSpec as P

MESH = pl.DeviceIdType.MESH
ROWS = 8
TILE = 64
HALF = TILE // 2
LANES = 128
PHASES = 6
AHEAD = 2


def merge_matrix(permute):
    out = np.zeros((2 * LANES, 2 * LANES), np.float32)
    for operand in range(2):
        for h in range(2):
            for c in range(TILE):
                place = (c % 2) * HALF + c // 2 if permute else c
                out[operand * LANES + h * TILE + c, h * LANES + operand * TILE + place] = 1.0
    return out


def untangle_matrix():
    out = np.zeros((LANES, LANES), np.float32)
    for j in range(2):
        for h in range(2):
            for p in range(HALF):
                out[j * TILE + h * HALF + p, j * TILE + 2 * p + h] = 1.0
    return out


def exchange(
    list_ref, amp_ref, int_ref, amat_ref, wmat_ref, own_ref, mir_ref,
    a_out, w_out, abuf, wbuf, o_out, obuf, mine, cbuf, mbuf,
    a_send, a_recv, f_send, f_recv, w_send, w_recv, o_send, o_recv, p_send, p_recv, keep, m_send, m_recv, n_send, n_recv,
):
    phases, _, span = a_out.shape[:3]
    occ = amp_ref.shape[0]
    slots = amp_ref.shape[2]
    half = slots // 2
    row = lax.axis_index("row")
    col = lax.axis_index("col")
    core = lax.rem(col, 2)
    other = 1 - core
    chip = col // 2
    y = chip // 2
    z = lax.rem(row, 4)
    xh, xl = lax.rem(chip, 2), row // 4
    x = xh * 2 + xl

    def spot(x_at, y_at, z_at, core_at):
        return {"row": lax.rem(x_at, 2) * 4 + z_at, "col": (y_at * 2 + x_at // 2) * 2 + core_at}

    y1 = y + 1 - 2 * lax.rem(y, 2)
    y3 = 3 - y
    x1 = x + 1 - 2 * lax.rem(x, 2)
    z0, zt = lax.rem(z, 2), z // 2
    y0, yt = lax.rem(y, 2), y // 2
    source = yt == xl
    turn = xh != z0
    leap = jnp.logical_or(xl != yt, y0 != zt)
    leg1 = (z0 * 2 + xl, y, zt * 2 + xh)
    leg2 = (xh * 2 + yt, xl * 2 + zt, y0 * 2 + z0)

    barrier = pltpu.get_barrier_semaphore()

    def greet(place):
        pl.semaphore_signal(barrier, inc=1, device_id=place, device_id_type=MESH)

    greet(spot(x, y, z, other))
    for step in range(1, 4):
        for e in range(2):
            greet(spot(lax.rem(x + step, 4), y, z, e))
            greet(spot(x, y, lax.rem(z + step, 4), e))
    greet(spot(x, y1, z, core))
    greet(spot(x, y3, z, core))

    @pl.when(turn)
    def _():
        greet(spot(*leg1, core))

    @pl.when(leap)
    def _():
        for e in range(2):
            greet(spot(*leg2, e))

    pl.semaphore_wait(barrier, 15 + jnp.where(turn, 1, 0) + jnp.where(leap, 2, 0))

    def remote(src, dst, send, recv, place):
        return pltpu.make_async_remote_copy(
            src_ref=src, dst_ref=dst, send_sem=send, recv_sem=recv, device_id=place, device_id_type=MESH
        )

    def arrived(buf, sem):
        pltpu.make_async_copy(buf, buf, sem).wait()

    def choose(cond, yes, no):
        pl.when(cond)(yes)
        pl.when(jnp.logical_not(cond))(no)

    def pack_a():
        for i in range(occ):
            left = amp_ref[i, 0].reshape(slots * HALF, LANES)
            right = amp_ref[i, 1].reshape(slots * HALF, LANES)
            both = jnp.concatenate([left, right], axis=1)
            made = jnp.dot(both, amat_ref[...], preferred_element_type=jnp.float32).astype(jnp.bfloat16)
            for s in range(slots):
                for h in range(2):
                    a_out[s % half // span, s // half, s % span, pl.ds(i * TILE + h * HALF, HALF), :] = made[
                        s * HALF : (s + 1) * HALF, h * LANES : (h + 1) * LANES
                    ]

    def pack_w(p):
        @pl.loop(0, 8)
        def _(r):
            xi, zd = r // 4, lax.rem(r, 4)
            for e in range(2):
                for u in range(span):
                    tile = list_ref[(r * slots + e * half + p * span + u) * 2 + 1]
                    left = int_ref[:, 0, tile].reshape(occ * HALF, LANES)
                    right = int_ref[:, 1, tile].reshape(occ * HALF, LANES)
                    both = jnp.concatenate([left, right], axis=1)
                    made = jnp.dot(both, wmat_ref[...], preferred_element_type=jnp.float32).astype(jnp.bfloat16)
                    for k in range(occ):
                        for g in range(2):
                            w_out[p, zd, e, u, xi, pl.ds(k * TILE + g * HALF, HALF), :] = made[
                                k * HALF : (k + 1) * HALF, g * LANES : (g + 1) * LANES
                            ]

    def send_a(p):
        for n in range(2):
            to = yt + 2 * n
            here = abuf.at[p, y0, x, core]

            def inside(n=n, here=here):
                remote(a_out.at[p, other], here, a_send.at[p, n, 0], a_recv.at[p, x, core], spot(x, y, z, other)).start()
                pltpu.make_async_copy(a_out.at[p, core], here, a_recv.at[p, x, core]).start()

            def outside(n=n, here=here, to=to):
                for e in range(2):
                    remote(a_out.at[p, e], here, a_send.at[p, n, e], a_recv.at[p, x, core], spot(to, y, z, e)).start()

            choose(to == x, inside, outside)

    def wait_a(p):
        for n in range(2):
            arrived(a_out.at[p, 0], a_send.at[p, n, 0])

            @pl.when(yt + 2 * n != x)
            def _(n=n):
                arrived(a_out.at[p, 0], a_send.at[p, n, 1])

    def w_copies(p):
        copies = []
        for step in (1, 3, 2):
            zd = lax.rem(z + step, 4)
            for e in range(2):
                copies.append(
                    remote(w_out.at[p, zd, e], wbuf.at[p, z, core], w_send.at[p, step, e], w_recv.at[p, z, core], spot(x, y, zd, e))
                )
        copies.append(
            remote(w_out.at[p, z, other], wbuf.at[p, z, core], w_send.at[p, 0, 0], w_recv.at[p, z, core], spot(x, y, z, other))
        )
        return copies

    def send_w(p):
        for copy in w_copies(p):
            copy.start()
        pltpu.make_async_copy(w_out.at[p, z, core], wbuf.at[p, z, core], w_recv.at[p, z, core]).start()

    first = jnp.where(source, y0, 1 - y0)
    second = 1 - first

    def forward(p):
        def take():
            for xs in range(4):
                for e in range(2):
                    arrived(abuf.at[p, first, xs, e], a_recv.at[p, xs, e])

        def wait():
            arrived(abuf.at[p, first], f_recv.at[p, first])

        choose(source, take, wait)
        remote(abuf.at[p, first], abuf.at[p, first], f_send.at[p, 0], f_recv.at[p, first], spot(x, y1, z, core)).start()

        @pl.when(source)
        def _():
            remote(abuf.at[p, first], abuf.at[p, first], f_send.at[p, 1], f_recv.at[p, first], spot(x, y3, z, core)).start()

    def wait_forward(p):
        arrived(abuf.at[p, first], f_send.at[p, 0])

        @pl.when(source)
        def _():
            arrived(abuf.at[p, first], f_send.at[p, 1])

    def compute(p):
        for zs in range(4):
            for e in range(2):
                arrived(wbuf.at[p, zs, e], w_recv.at[p, zs, e])
        arrived(abuf.at[p, second], f_recv.at[p, second])
        for theirs in (True, False):
            xi = 1 - xl if theirs else xl

            @pl.loop(0, span)
            def _(u, xi=xi, theirs=theirs):
                total = jnp.zeros((4 * TILE, 4 * TILE), jnp.float32)
                for zs in range(4):
                    xs = (zs % 2) * 2 + xi
                    left = jnp.concatenate([abuf[p, zs // 2, xs, 0, u], abuf[p, zs // 2, xs, 1, u]], axis=1)
                    right = jnp.concatenate([wbuf[p, zs, 0, u, xi], wbuf[p, zs, 1, u, xi]], axis=1)
                    total = total + jnp.dot(left, right, preferred_element_type=jnp.float32)
                if theirs:
                    o_out[p, u] = total
                else:
                    mine[p, u] = total

            if theirs:
                o_copy(p).start()

    def o_copy(p):
        return remote(o_out.at[p], obuf.at[p], o_send.at[p], o_recv.at[p], spot(x1, y, z, core))

    def p_copy(p):
        return remote(cbuf.at[p, :, other], own_ref.at[core, p], p_send.at[p], p_recv.at[p], spot(x, y, z, other))

    def k_copy(p):
        return pltpu.make_async_copy(cbuf.at[p, :, core], own_ref.at[core, p], keep.at[p])

    def m_copy(p):
        return remote(cbuf.at[p], mbuf.at[p], m_send.at[p], m_recv.at[p], spot(*leg1, core))

    def n_copy(p, q, place):
        return remote(mbuf.at[p, q], mir_ref.at[core, p], n_send.at[p, q], n_recv.at[p, core], place)

    def add(p):
        arrived(obuf.at[p], o_recv.at[p])

        @pl.loop(0, span)
        def _(u):
            made = (mine[p, u] + obuf[p, u]).astype(jnp.bfloat16)
            for q in range(2):
                for j in range(2):
                    cbuf[p, q, j, u] = made[q * LANES : (q + 1) * LANES, j * LANES : (j + 1) * LANES]

        def stay():
            pltpu.make_async_copy(cbuf.at[p], mbuf.at[p], m_recv.at[p]).start()

        choose(turn, lambda: m_copy(p).start(), stay)
        p_copy(p).start()
        k_copy(p).start()

    def relay(p):
        arrived(mbuf.at[p], m_recv.at[p])

        def away():
            for q in range(2):
                n_copy(p, q, spot(*leg2, q)).start()

        def within():
            n_copy(p, other, spot(x, y, z, other)).start()
            pltpu.make_async_copy(mbuf.at[p, core], mir_ref.at[core, p], n_recv.at[p, core]).start()

        choose(leap, away, within)

    def close(p):
        for e in range(2):
            arrived(mir_ref.at[e, p], n_recv.at[p, e])
        arrived(own_ref.at[other, p], p_recv.at[p])
        k_copy(p).wait()
        p_copy(p).wait_send()
        o_copy(p).wait_send()
        pl.when(turn)(lambda: m_copy(p).wait_send())

        def away():
            for q in range(2):
                arrived(mbuf.at[p, q], n_send.at[p, q])

        def within():
            arrived(mbuf.at[p, other], n_send.at[p, other])

        choose(leap, away, within)
        wait_a(p)
        wait_forward(p)
        for copy in w_copies(p):
            copy.wait_send()

    def issue(p):
        send_a(p)
        pack_w(p)
        send_w(p)

    pack_a()
    for p in range(min(AHEAD, phases)):
        issue(p)
    forward(0)
    for p in range(phases):
        if p + AHEAD < phases:
            issue(p + AHEAD)
        if p + 1 < phases:
            forward(p + 1)
        compute(p)
        if p >= 1:
            add(p - 1)
        if p >= 2:
            relay(p - 2)
    add(phases - 1)
    if phases >= 2:
        relay(phases - 2)
    relay(phases - 1)
    for p in range(phases):
        close(p)


def finish(list_ref, count_ref, own_ref, mir_ref, mat_ref, out_ref, turn):
    slots = out_ref.shape[2]
    half = slots // 2
    span = own_ref.shape[3]
    row = lax.axis_index("row")
    partner = lax.axis_index("col") // 2
    live_count = count_ref[row]
    their_count = count_ref[partner]
    lane = lax.broadcasted_iota(jnp.int32, (HALF, LANES), 1)
    low = lane < TILE

    def fold(even, odd):
        first = jnp.where(low, even, pltpu.roll(odd, TILE, 1))
        second = jnp.where(low, pltpu.roll(even, TILE, 1), odd)
        return first, second

    @pl.loop(0, slots)
    def _(s):
        live = (s < live_count).astype(jnp.float32)
        a = list_ref[(row * slots + s) * 2]
        b = list_ref[(row * slots + s) * 2 + 1]
        found = jnp.int32(-1)
        for t in range(slots):
            same = (list_ref[(partner * slots + t) * 2] == b) & (list_ref[(partner * slots + t) * 2 + 1] == a)
            found = jnp.where(same & (t < their_count), t, found)
        hit = (found >= 0).astype(jnp.float32)
        t = jnp.maximum(found, 0)
        te, tp, tu = t // half, lax.rem(t, half) // span, lax.rem(t, span)
        se, sp, su = s // half, lax.rem(s, half) // span, lax.rem(s, span)
        for jp in range(2):
            block = mir_ref[te, tp, jp, tu]
            turned = lax.dot_general(block, mat_ref[...], (((0,), (0,)), ((), ())), preferred_element_type=jnp.float32)
            turn[...] = turned * hit
            for u in range(2):
                i = jp * 2 + u
                even = turn[pl.ds(u * TILE, HALF, stride=2), :]
                odd = turn[pl.ds(u * TILE + 1, HALF, stride=2), :]
                mine = own_ref[se, sp, jp, su]
                top = mine[u * TILE : u * TILE + HALF].astype(jnp.float32)
                bottom = mine[u * TILE + HALF : (u + 1) * TILE].astype(jnp.float32)
                first, second = fold((top + even) * live, (bottom + odd) * live)
                out_ref[i, 0, s] = first
                out_ref[i, 1, s] = second


def on_device(amplitudes, integrals, pair_lists, tile_counts):
    occ_row, occ_col, slots, square = amplitudes.shape
    half = slots // 2
    span = half // PHASES
    tiles = integrals.shape[2]
    bf16 = jnp.bfloat16
    f32 = jnp.float32
    block = occ_row * TILE
    vmem = pl.BlockSpec(memory_space=pltpu.VMEM)
    smem = pl.BlockSpec(memory_space=pltpu.SMEM)
    anywhere = pl.BlockSpec(memory_space=pl.ANY)
    dma = pltpu.SemaphoreType.DMA

    lists = pair_lists.reshape(-1)
    amp = amplitudes.reshape(occ_row, occ_col, slots, HALF, LANES)
    integ = integrals.reshape(occ_row, occ_col, tiles, HALF, LANES)

    own, mirror = pl.pallas_call(
        exchange,
        name="exchange",
        out_shape=(
            jax.ShapeDtypeStruct((2, PHASES, 2, span, LANES, LANES), bf16),
            jax.ShapeDtypeStruct((2, PHASES, 2, span, LANES, LANES), bf16),
        ),
        in_specs=[smem, vmem, vmem, vmem, vmem],
        out_specs=(anywhere, anywhere),
        scratch_shapes=[
            pltpu.VMEM((PHASES, 2, span, block, LANES), bf16),
            pltpu.VMEM((PHASES, 4, 2, span, 2, block, LANES), bf16),
            pltpu.VMEM((PHASES, 2, 4, 2, span, block, LANES), bf16),
            pltpu.VMEM((PHASES, 4, 2, span, 2, block, LANES), bf16),
            pltpu.VMEM((PHASES, span, block, 2 * LANES), f32),
            pltpu.VMEM((PHASES, span, block, 2 * LANES), f32),
            pltpu.VMEM((PHASES, span, block, 2 * LANES), f32),
            pltpu.VMEM((PHASES, 2, 2, span, LANES, LANES), bf16),
            pltpu.VMEM((PHASES, 2, 2, span, LANES, LANES), bf16),
            dma((PHASES, 2, 2)),
            dma((PHASES, 4, 2)),
            dma((PHASES, 2)),
            dma((PHASES, 2)),
            dma((PHASES, 4, 2)),
            dma((PHASES, 4, 2)),
            dma((PHASES,)),
            dma((PHASES,)),
            dma((PHASES,)),
            dma((PHASES,)),
            dma((PHASES,)),
            dma((PHASES,)),
            dma((PHASES,)),
            dma((PHASES, 2)),
            dma((PHASES, 2)),
        ],
        compiler_params=pltpu.CompilerParams(collective_id=0, has_side_effects=True, vmem_limit_bytes=48 << 20),
    )(lists, amp, integ, jnp.asarray(merge_matrix(True), bf16), jnp.asarray(merge_matrix(False), bf16))

    packed = pl.pallas_call(
        finish,
        name="finish",
        out_shape=jax.ShapeDtypeStruct((occ_row, occ_col, slots, HALF, LANES), f32),
        in_specs=[smem, smem, vmem, vmem, vmem],
        out_specs=vmem,
        scratch_shapes=[pltpu.VMEM((LANES, LANES), f32)],
        compiler_params=pltpu.CompilerParams(vmem_limit_bytes=32 << 20),
    )(lists, tile_counts, own, mirror, jnp.asarray(untangle_matrix(), bf16))
    return packed.reshape(occ_row, occ_col, slots, square)


def solution(mesh):
    return jax.shard_map(
        on_device,
        mesh=mesh,
        in_specs=(P("row", "col", None, None), P("row", "col", None, None), P(), P()),
        out_specs=P("row", "col", None, None),
        check_vma=False,
    )
```

time: 509 us -> 170 us (0.33)
  the two profiles are of different devices: /device:TPU:3 before, /device:TPU:29 now
where the time goes in v2:
time: 170 us; the launch traced here: 169 us
  Pallas kernels  151 us (89%)
  local copies, waits for them, and re-layouts  18.1 us (11%)
    pallas_call x1, Pallas kernels, on_device(): pl.pallas_call(exchange, name='exchange', out_shape=(jax.ShapeDtypeStruct...  146 us
    reshape x2, local copies, waits for them, and re-layouts, on_device(): integ = integrals.reshape(occ_row, occ_col, tiles, HALF, LANES)  10.6 us
    pallas_call x1, Pallas kernels, on_device(): pl.pallas_call(finish, name='finish', out_shape=jax.ShapeDtypeStruct((occ...  4.7 us
    reshape x2, local copies, waits for them, and re-layouts, on_device(): amp = amplitudes.reshape(occ_row, occ_col, slots, HALF, LANES)  4.47 us

profile of v2, /device:TPU:29, one launch (start us, length us, event | category | flops | bytes accessed | tf_op | source)
XLA Modules:
  0.0 169.4 jit_solution(18286818202904780576)
XLA Ops:
  0.0 0.8 copy.11
  0.8 0.1 reshape.12.list_ref
  1.0 8.1 %reshape.16 = bf16[4,2,47,32,128]{4,3,1,2,0:T(8,128)(2,1)} reshape(bf16[4,2,47,4096]{3,1,2,0:T(2,128)(2,1)} %param.8) | data formatting | bytes 6160384 | tf_op jit(solution)/shard_map/reshape | solution.py:382
  9.1 2.4 %copy.15.int_ref = bf16[4,2,47,32,128]{4,3,2,1,0:T(8,128)(2,1)S(1)} copy(bf16[4,2,47,32,128]{4,3,1,2,0:T(8,128)(2,1)} %reshape.16) | data formatting | bytes 6160384 | tf_op jit(solution)/shard_map/reshape | solution.py:382
  11.5 0.0 copy-start
  11.6 0.0 copy-start.1
  11.6 3.3 %reshape.13 = bf16[4,2,12,32,128]{4,3,1,2,0:T(8,128)(2,1)} reshape(bf16[4,2,12,4096]{3,1,2,0:T(2,128)(2,1)} %param.7) | data formatting | bytes 1572864 | tf_op jit(solution)/shard_map/reshape | solution.py:381
  14.8 0.0 copy-start.2
  14.8 0.0 copy-start.3
  14.8 1.2 copy.13.amp_ref
  16.1 0.0 copy-done
  16.1 0.0 copy-done.1
  16.1 146.5 %exchange.1 = (bf16[2,6,2,1,128,128]{5,4,3,2,1,0:T(8,128)(2,1)S(1)}, bf16[2,6,2,1,128,128]{5,4,3,2,1,0:T(8,128)(2,1)S(1)}) custom-call(s32[192]{0:T(256)S(1)} %reshape.12.list_ref, bf16[4,2,12,32,128]{4,3,2,1,0:T(8,128)(2,1)S(1)} %copy.13.amp_ref, bf16[4,2,47,32,128]{4,3,2,1,0:T(8,128)(2,1)S(1)} %copy.15.int_ref, bf16[256,256]{1,0:T(8,128)(2,1)S(1)} %copy-done, ...), custom_call_target="tpu_custom_call" | custom-call | tf_op jit(solution)/shard_map/exchange/pallas_call | solution.py:384
  162.6 0.0 copy-done.2
  162.6 0.0 copy-done.3
  162.6 4.7 %finish.1 = f32[4,2,12,32,128]{4,3,2,1,0:T(8,128)S(1)} custom-call(s32[192]{0:T(256)S(1)} %reshape.12.list_ref, s32[8]{0:T(128)S(1)} %copy-done.3, bf16[2,6,2,1,128,128]{5,4,3,2,1,0:T(8,128)(2,1)S(1)} %get-tuple-element.7.own_ref, bf16[2,6,2,1,128,128]{5,4,3,2,1,0:T(8,128)(2,1)S(1)} %get-tuple-element.8.mir_ref, bf16[128,128]{1,0:T(8,128)(2,1)S(1)} %copy-done.2), custom_call_target="tpu_custom_call" | custom-call | tf_op jit(solution)/shard_map/finish/pallas_call | solution.py:422
  167.3 0.1 copy.14
  167.4 2.0 %reshape.15 = f32[4,2,12,4096]{3,1,2,0:T(2,128)} reshape(f32[4,2,12,32,128]{4,3,1,2,0:T(8,128)S(1)} %copy.14) | data formatting | bytes 3145728 | tf_op jit(solution)/shard_map/reshape | solution.py:431
Async XLA Ops:
  11.5 4.5 %copy-start = (bf16[256,256]{1,0:T(8,128)(2,1)S(1)}, bf16[256,256]{1,0:T(8,128)(2,1)}, u32[]{:S(2)}) copy-start(bf16[256,256]{1,0:T(8,128)(2,1)} %constant.6.clone.amat_ref) | copy-start | bytes 393220
  11.6 4.5 %copy-start.1 = (bf16[256,256]{1,0:T(8,128)(2,1)S(1)}, bf16[256,256]{1,0:T(8,128)(2,1)}, u32[]{:S(2)}) copy-start(bf16[256,256]{1,0:T(8,128)(2,1)} %constant.7.clone.wmat_ref) | copy-start | bytes 393220
  14.8 147.7 %copy-start.2 = (bf16[128,128]{1,0:T(8,128)(2,1)S(1)}, bf16[128,128]{1,0:T(8,128)(2,1)}, u32[]{:S(2)}) copy-start(bf16[128,128]{1,0:T(8,128)(2,1)} %constant.8.clone.mat_ref) | copy-start | bytes 98308
  14.8 147.7 %copy-start.3 = (s32[8]{0:T(128)S(1)}, s32[8]{0:T(128)}, u32[]{:S(2)}) copy-start(s32[8]{0:T(128)} %count_ref.1) | copy-start | bytes 100

commit v3 on v2

v3 whole, which is shorter than its diff:
```python
import functools

import jax
import jax.numpy as jnp
import numpy as np
from jax import lax
from jax.experimental import pallas as pl
from jax.experimental.pallas import tpu as pltpu
from jax.sharding import PartitionSpec as P

MESH = pl.DeviceIdType.MESH
ROWS = 8
TILE = 64
HALF = TILE // 2
LANES = 128
PHASES = 6
A_AHEAD = 3
W_AHEAD = 3
LAG = 2
RELAYS = (
    (0, 51, 48, 55, 5, 58, 3, 59, 7, 49, 38, 4, 11, 50, 6, 54, 18, 44, 43, 36, 42, 27, 20, 47, 24, 52, 28, 16, 46, 40, 22, 45, 23, 35, 17, 41, 34, 39, 25, 19, 29, 37, 21, 32, 31, 2, 30, 33, 13, 61, 12, 62, 9, 26, 14, 53, 8, 60, 1, 57, 10, 56, 15, 63),
    (3, 0, 5, 2, 50, 62, 53, 54, 8, 60, 48, 59, 1, 63, 6, 57, 32, 41, 44, 28, 42, 22, 29, 34, 40, 43, 16, 58, 31, 47, 46, 23, 17, 26, 38, 24, 45, 35, 7, 20, 33, 21, 25, 37, 19, 36, 18, 39, 4, 9, 14, 30, 11, 56, 15, 51, 10, 61, 49, 13, 27, 55, 12, 52),
    (14, 56, 0, 53, 62, 9, 10, 49, 59, 48, 5, 8, 3, 7, 54, 51, 21, 46, 44, 36, 57, 42, 30, 27, 20, 40, 43, 28, 17, 24, 39, 19, 29, 33, 23, 37, 16, 35, 22, 32, 25, 45, 34, 38, 18, 31, 47, 41, 26, 12, 2, 60, 6, 63, 4, 55, 13, 58, 61, 1, 52, 50, 15, 11),
    (1, 45, 8, 63, 60, 6, 53, 37, 52, 51, 4, 48, 2, 14, 49, 54, 24, 20, 19, 46, 31, 29, 35, 44, 27, 18, 58, 30, 26, 41, 25, 42, 22, 32, 10, 40, 47, 21, 38, 39, 17, 33, 16, 36, 28, 34, 23, 43, 9, 50, 61, 57, 56, 5, 12, 15, 7, 59, 62, 0, 11, 55, 13, 3),
    (8, 48, 5, 52, 6, 15, 54, 58, 4, 57, 3, 53, 14, 34, 39, 51, 63, 43, 21, 47, 25, 30, 26, 61, 37, 36, 44, 29, 40, 46, 19, 50, 17, 18, 41, 33, 27, 16, 20, 22, 45, 42, 28, 23, 35, 32, 24, 38, 2, 9, 13, 49, 56, 7, 10, 12, 31, 1, 0, 60, 55, 59, 62, 11),
    (0, 48, 4, 54, 15, 59, 7, 51, 58, 56, 3, 52, 2, 62, 57, 10, 28, 43, 24, 47, 30, 41, 27, 42, 29, 33, 18, 31, 26, 25, 34, 46, 16, 17, 20, 38, 35, 45, 40, 23, 32, 39, 37, 21, 22, 19, 36, 44, 49, 8, 1, 13, 55, 11, 63, 50, 5, 53, 9, 61, 14, 6, 60, 12),
)


def merge_matrix(permute):
    out = np.zeros((2 * LANES, 2 * LANES), np.float32)
    for operand in range(2):
        for h in range(2):
            for c in range(TILE):
                place = (c % 2) * HALF + c // 2 if permute else c
                out[operand * LANES + h * TILE + c, h * LANES + operand * TILE + place] = 1.0
    return out


def untangle_matrix():
    out = np.zeros((LANES, LANES), np.float32)
    for j in range(2):
        for h in range(2):
            for p in range(HALF):
                out[j * TILE + h * HALF + p, j * TILE + 2 * p + h] = 1.0
    return out


def exchange(
    list_ref, count_ref, amp_ref, int_ref, amat_ref, wmat_ref, own_ref, mir_ref, at_ref,
    a_out, w_out, abuf, wbuf, cbuf, mbuf,
    y_send, y_recv, x_send, v_send, v_recv, p_send, p_recv, keep, m_send, m_recv, n_send, n_recv,
):
    phases, _, span = a_out.shape[:3]
    occ = amp_ref.shape[0]
    slots = amp_ref.shape[2]
    half = slots // 2
    row = lax.axis_index("row")
    col = lax.axis_index("col")
    core = lax.rem(col, 2)
    other = 1 - core
    chip = col // 2
    y = chip // 2
    z = lax.rem(row, 4)
    xh, xl = lax.rem(chip, 2), row // 4
    x = xh * 2 + xl

    def place_of(c, core_at):
        return spot(c // 16, c // 4 % 4, c % 4, core_at)

    def spot(x_at, y_at, z_at, core_at):
        return {"row": lax.rem(x_at, 2) * 4 + z_at, "col": (y_at * 2 + x_at // 2) * 2 + core_at}

    x1 = x + 1 - 2 * lax.rem(x, 2)
    x2 = lax.rem(x + 2, 4)

    def mirror_of(c):
        xa, ya, za = c // 16, c // 4 % 4, c % 4
        return (za % 2 * 2 + ya // 2) * 16 + (xa % 2 * 2 + za // 2) * 4 + ya % 2 * 2 + xa // 2

    def look(table, at):
        value = jnp.int32(table[0])
        for n in range(1, len(table)):
            value = jnp.where(at == n, table[n], value)
        return value

    def inverse(table):
        turned = [0] * len(table)
        for n, v in enumerate(table):
            turned[v] = n
        return turned

    here = x * 16 + y * 4 + z
    goes = [look(table, here) for table in RELAYS]
    comes = [look(inverse(table), here) for table in RELAYS]
    ends = [mirror_of(c) for c in comes]
    hands = [look(table, mirror_of(here)) for table in RELAYS]

    barrier = pltpu.get_barrier_semaphore()

    def greet(place):
        pl.semaphore_signal(barrier, inc=1, device_id=place, device_id_type=MESH)

    greet(spot(x, y, z, other))
    for step in range(1, 4):
        for e in range(2):
            greet(spot(lax.rem(x + step, 4), y, z, e))
            greet(spot(x, y, lax.rem(z + step, 4), e))
    for step in range(1, 4):
        for e in range(2):
            greet(spot(x, lax.rem(y + step, 4), z, e))
            greet(spot(x1, y, lax.rem(z + step, 4), e))

    total = jnp.int32(25)
    for n in range(len(RELAYS)):
        @pl.when(comes[n] != here)
        def _(n=n):
            greet(place_of(comes[n], core))

        @pl.when(hands[n] != here)
        def _(n=n):
            for e in range(2):
                greet(place_of(hands[n], e))

        total = total + jnp.where(goes[n] != here, 1, 0) + jnp.where(ends[n] != here, 2, 0)

    pl.semaphore_wait(barrier, total)

    def remote(src, dst, send, recv, place):
        return pltpu.make_async_remote_copy(
            src_ref=src, dst_ref=dst, send_sem=send, recv_sem=recv, device_id=place, device_id_type=MESH
        )

    def arrived(buf, sem):
        pltpu.make_async_copy(buf, buf, sem).wait()

    def choose(cond, yes, no):
        pl.when(cond)(yes)
        pl.when(jnp.logical_not(cond))(no)

    def pack_a():
        for i in range(occ):
            left = amp_ref[i, 0].reshape(slots * HALF, LANES)
            right = amp_ref[i, 1].reshape(slots * HALF, LANES)
            both = jnp.concatenate([left, right], axis=1)
            made = jnp.dot(both, amat_ref[...], preferred_element_type=jnp.float32).astype(jnp.bfloat16)
            for s in range(slots):
                for h in range(2):
                    a_out[s % half // span, s // half, s % span, pl.ds(i * TILE + h * HALF, HALF), :] = made[
                        s * HALF : (s + 1) * HALF, h * LANES : (h + 1) * LANES
                    ]

    def pack_w(p):
        @pl.loop(0, 8)
        def _(r):
            xi, zd = r // 4, lax.rem(r, 4)
            for e in range(2):
                for u in range(span):
                    tile = list_ref[(r * slots + e * half + p * span + u) * 2 + 1]
                    left = int_ref[:, 0, tile].reshape(occ * HALF, LANES)
                    right = int_ref[:, 1, tile].reshape(occ * HALF, LANES)
                    both = jnp.concatenate([left, right], axis=1)
                    made = jnp.dot(both, wmat_ref[...], preferred_element_type=jnp.float32).astype(jnp.bfloat16)
                    for k in range(occ):
                        for g in range(2):
                            w_out[p, zd, e, u, xi, pl.ds(k * TILE + g * HALF, HALF), :] = made[
                                k * HALF : (k + 1) * HALF, g * LANES : (g + 1) * LANES
                            ]

    def y_copies(p):
        n = p
        here = abuf.at[p, xh, y, core]
        copies = []
        for e in range(2):
            copies.append(remote(a_out.at[p, e], here, y_send.at[n, 4, e], y_recv.at[n, xh, y, core], spot(x2, y, z, e)))
        for step in (1, 3, 2):
            for e in range(2):
                place = spot(x, lax.rem(y + step, 4), z, e)
                copies.append(remote(a_out.at[p, e], here, y_send.at[n, step, e], y_recv.at[n, xh, y, core], place))
        copies.append(remote(a_out.at[p, other], here, y_send.at[n, 0, 0], y_recv.at[n, xh, y, core], spot(x, y, z, other)))
        return copies

    def send_y(p):
        for copy in y_copies(p):
            copy.start()
        n = p
        pltpu.make_async_copy(a_out.at[p, core], abuf.at[p, xh, y, core], y_recv.at[n, xh, y, core]).start()

    def pass_copies(p):
        n = p
        copies = []
        for step in (1, 3, 2):
            for e in range(2):
                block = abuf.at[p, 1 - xh, y, e]
                place = spot(x, lax.rem(y + step, 4), z, core)
                copies.append(remote(block, block, x_send.at[n, step, e], y_recv.at[n, 1 - xh, y, e], place))
        return copies

    def pass_on(p):
        n = p
        for e in range(2):
            arrived(abuf.at[p, 1 - xh, y, e], y_recv.at[n, 1 - xh, y, e])
        for copy in pass_copies(p):
            copy.start()

    def v_copies(p):
        n = p
        copies = []
        for flip in (1, 0):
            for step in (1, 3, 2, 0):
                zd = lax.rem(z + step, 4)
                to = lax.rem(xl + flip, 2)
                for e in range(2):
                    if flip or step:
                        place = spot(xh * 2 + to, y, zd, e)
                        copies.append(
                            remote(
                                w_out.at[p, zd, e, :, to], wbuf.at[p, z, core, :, xl],
                                v_send.at[n, flip, step, e], v_recv.at[n, z, core, xl], place,
                            )
                        )
        copies.append(
            remote(
                w_out.at[p, z, other, :, xl], wbuf.at[p, z, core, :, xl],
                v_send.at[n, 0, 0, 0], v_recv.at[n, z, core, xl], spot(x, y, z, other),
            )
        )
        return copies

    def send_v(p):
        for copy in v_copies(p):
            copy.start()
        n = p
        pltpu.make_async_copy(
            w_out.at[p, z, core, :, xl], wbuf.at[p, z, core, :, xl], v_recv.at[n, z, core, xl]
        ).start()

    def compute(p):
        n = p
        for a in range(2):
            for b in range(4):
                for e in range(2):

                    @pl.when(jnp.logical_or(a == xh, b != y))
                    def _(a=a, b=b, e=e):
                        arrived(abuf.at[p, a, b, e], y_recv.at[n, a, b, e])

        for zs in range(4):
            for e in range(2):
                for ks in range(2):
                    arrived(wbuf.at[p, zs, e, :, ks], v_recv.at[n, zs, e, ks])

        @pl.loop(0, span)
        def _(u):
            total = jnp.zeros((4 * TILE, 4 * TILE), jnp.float32)
            for zs in range(4):
                for ks in range(2):
                    b = ks * 2 + zs // 2
                    left = jnp.concatenate([abuf[p, zs % 2, b, 0, u], abuf[p, zs % 2, b, 1, u]], axis=1)
                    right = jnp.concatenate([wbuf[p, zs, 0, u, ks], wbuf[p, zs, 1, u, ks]], axis=1)
                    total = total + jnp.dot(left, right, preferred_element_type=jnp.float32)
            keep_sum(p, u, total)

        emit(p)

    def p_copy(p):
        return remote(cbuf.at[p, :, other], own_ref.at[core, p], p_send.at[p], p_recv.at[p], spot(x, y, z, other))

    def k_copy(p):
        return pltpu.make_async_copy(cbuf.at[p, :, core], own_ref.at[core, p], keep.at[p])

    def m_copy(p):
        return remote(cbuf.at[p], mbuf.at[p], m_send.at[p], m_recv.at[p], place_of(goes[p % len(RELAYS)], core))

    def n_copy(p, q, place):
        return remote(mbuf.at[p, q], mir_ref.at[core, p], n_send.at[p, q], n_recv.at[p, core], place)

    def keep_sum(p, u, total):
        made = total.astype(jnp.bfloat16)
        for q in range(2):
            for j in range(2):
                cbuf[p, q, j, u] = made[q * LANES : (q + 1) * LANES, j * LANES : (j + 1) * LANES]

    def emit(p):
        def stay():
            pltpu.make_async_copy(cbuf.at[p], mbuf.at[p], m_recv.at[p]).start()

        choose(goes[p % len(RELAYS)] != here, lambda: m_copy(p).start(), stay)
        p_copy(p).start()
        k_copy(p).start()

    def relay(p):
        arrived(mbuf.at[p], m_recv.at[p])

        def away():
            for q in range(2):
                n_copy(p, q, place_of(ends[p % len(RELAYS)], q)).start()

        def within():
            n_copy(p, other, spot(x, y, z, other)).start()
            pltpu.make_async_copy(mbuf.at[p, core], mir_ref.at[core, p], n_recv.at[p, core]).start()

        choose(ends[p % len(RELAYS)] != here, away, within)

    def close(p):
        for e in range(2):
            arrived(mir_ref.at[e, p], n_recv.at[p, e])
        arrived(own_ref.at[other, p], p_recv.at[p])
        k_copy(p).wait()
        p_copy(p).wait_send()
        pl.when(goes[p % len(RELAYS)] != here)(lambda: m_copy(p).wait_send())

        def away():
            for q in range(2):
                arrived(mbuf.at[p, q], n_send.at[p, q])

        def within():
            arrived(mbuf.at[p, other], n_send.at[p, other])

        choose(ends[p % len(RELAYS)] != here, away, within)
        for copy in y_copies(p) + pass_copies(p) + v_copies(p):
            copy.wait_send()

    def find():
        for s in range(slots):
            a = list_ref[(row * slots + s) * 2]
            b = list_ref[(row * slots + s) * 2 + 1]
            found = jnp.int32(-1)
            for t in range(slots):
                same = (list_ref[(chip * slots + t) * 2] == b) & (list_ref[(chip * slots + t) * 2 + 1] == a)
                found = jnp.where(same & (t < count_ref[chip]), t, found)
            at_ref[0, s] = jnp.maximum(found, 0)
            at_ref[1, s] = (found >= 0).astype(jnp.int32)
            at_ref[2, s] = (s < count_ref[row]).astype(jnp.int32)

    pack_a()
    for p in range(min(A_AHEAD, phases)):
        send_y(p)
    for p in range(min(W_AHEAD, phases)):
        pack_w(p)
        send_v(p)
        if p == 0:
            pass_on(0)
    find()
    for p in range(phases):
        if p + A_AHEAD < phases:
            send_y(p + A_AHEAD)
        if p + 1 < phases:
            pass_on(p + 1)
        if p + W_AHEAD < phases:
            pack_w(p + W_AHEAD)
            send_v(p + W_AHEAD)
        compute(p)
        if p >= LAG:
            relay(p - LAG)
    for p in range(max(phases - LAG, 0), phases):
        relay(p)
    for p in range(phases):
        close(p)


def finish(at_ref, own_ref, mir_ref, mat_ref, out_ref, turn):
    slots = out_ref.shape[2]
    half = slots // 2
    span = own_ref.shape[3]
    lane = lax.broadcasted_iota(jnp.int32, (HALF, LANES), 1)
    low = lane < TILE

    def fold(even, odd):
        first = jnp.where(low, even, pltpu.roll(odd, TILE, 1))
        second = jnp.where(low, pltpu.roll(even, TILE, 1), odd)
        return first, second

    for s in range(slots):
        t = at_ref[0, s]
        hit = at_ref[1, s].astype(jnp.float32)
        live = at_ref[2, s].astype(jnp.float32)
        te, tp, tu = t // half, lax.rem(t, half) // span, lax.rem(t, span)
        se, sp, su = s // half, s % half // span, s % span
        for jp in range(2):
            block = mir_ref[te, tp, jp, tu]
            turned = lax.dot_general(block, mat_ref[...], (((0,), (0,)), ((), ())), preferred_element_type=jnp.float32)
            turn[s % 2, jp] = turned * hit
            mine = own_ref[se, sp, jp, su].astype(jnp.float32)
            for u in range(2):
                i = jp * 2 + u
                even = turn[s % 2, jp, pl.ds(u * TILE, HALF, stride=2), :]
                odd = turn[s % 2, jp, pl.ds(u * TILE + 1, HALF, stride=2), :]
                top = mine[u * TILE : u * TILE + HALF]
                bottom = mine[u * TILE + HALF : (u + 1) * TILE]
                first, second = fold((top + even) * live, (bottom + odd) * live)
                out_ref[i, 0, s] = first
                out_ref[i, 1, s] = second


def on_device(amplitudes, integrals, pair_lists, tile_counts):
    occ_row, occ_col, slots, square = amplitudes.shape
    half = slots // 2
    span = half // PHASES
    tiles = integrals.shape[2]
    bf16 = jnp.bfloat16
    f32 = jnp.float32
    block = occ_row * TILE
    vmem = pl.BlockSpec(memory_space=pltpu.VMEM)
    smem = pl.BlockSpec(memory_space=pltpu.SMEM)
    anywhere = pl.BlockSpec(memory_space=pl.ANY)
    dma = pltpu.SemaphoreType.DMA

    lists = pair_lists.reshape(-1)
    amp = amplitudes.reshape(occ_row, occ_col, slots, HALF, LANES)
    integ = integrals.reshape(occ_row, occ_col, tiles, HALF, LANES)

    own, mirror, places = pl.pallas_call(
        exchange,
        name="exchange",
        out_shape=(
            jax.ShapeDtypeStruct((2, PHASES, 2, span, LANES, LANES), bf16),
            jax.ShapeDtypeStruct((2, PHASES, 2, span, LANES, LANES), bf16),
            jax.ShapeDtypeStruct((3, slots), jnp.int32),
        ),
        in_specs=[smem, smem, vmem, vmem, vmem, vmem],
        out_specs=(anywhere, anywhere, smem),
        scratch_shapes=[
            pltpu.VMEM((PHASES, 2, span, block, LANES), bf16),
            pltpu.VMEM((PHASES, 4, 2, span, 2, block, LANES), bf16),
            pltpu.VMEM((PHASES, 2, 4, 2, span, block, LANES), bf16),
            pltpu.VMEM((PHASES, 4, 2, span, 2, block, LANES), bf16),
            pltpu.VMEM((PHASES, 2, 2, span, LANES, LANES), bf16),
            pltpu.VMEM((PHASES, 2, 2, span, LANES, LANES), bf16),
            dma((PHASES, 5, 2)),
            dma((PHASES, 2, 4, 2)),
            dma((PHASES, 4, 2)),
            dma((PHASES, 2, 4, 2)),
            dma((PHASES, 4, 2, 2)),
            dma((PHASES,)),
            dma((PHASES,)),
            dma((PHASES,)),
            dma((PHASES,)),
            dma((PHASES,)),
            dma((PHASES, 2)),
            dma((PHASES, 2)),
        ],
        compiler_params=pltpu.CompilerParams(collective_id=0, has_side_effects=True, vmem_limit_bytes=48 << 20),
    )(lists, tile_counts, amp, integ, jnp.asarray(merge_matrix(True), bf16), jnp.asarray(merge_matrix(False), bf16))

    packed = pl.pallas_call(
        finish,
        name="finish",
        out_shape=jax.ShapeDtypeStruct((occ_row, occ_col, slots, HALF, LANES), f32),
        in_specs=[smem, vmem, vmem, vmem],
        out_specs=vmem,
        scratch_shapes=[pltpu.VMEM((2, 2, LANES, LANES), f32)],
        compiler_params=pltpu.CompilerParams(vmem_limit_bytes=32 << 20),
    )(places, own, mirror, jnp.asarray(untangle_matrix(), bf16))
    return packed.reshape(occ_row, occ_col, slots, square)


def solution(mesh):
    return jax.shard_map(
        on_device,
        mesh=mesh,
        in_specs=(P("row", "col", None, None), P("row", "col", None, None), P(), P()),
        out_specs=P("row", "col", None, None),
        check_vma=False,
    )
```

time: 170 us -> 148 us (0.87)
  the two profiles are of different devices: /device:TPU:29 before, /device:TPU:3 now
where the time goes in v3:
time: 148 us
  Pallas kernels  128 us (86%)
  local copies, waits for them, and re-layouts  19.5 us (13%)
    pallas_call x1, Pallas kernels, on_device(): pl.pallas_call(exchange, name='exchange', out_shape=(jax.ShapeDtypeStruct...  127 us
    reshape x2, local copies, waits for them, and re-layouts, on_device(): integ = integrals.reshape(occ_row, occ_col, tiles, HALF, LANES)  10.6 us
    reshape x2, local copies, waits for them, and re-layouts, on_device(): amp = amplitudes.reshape(occ_row, occ_col, slots, HALF, LANES)  5.4 us

profile of v3, /device:TPU:3, one launch (start us, length us, event | category | flops | bytes accessed | tf_op | source)
XLA Modules:
  0.0 147.6 jit_solution(7636325019494197292)
XLA Ops:
  0.0 8.1 %reshape.16 = bf16[4,2,47,32,128]{4,3,1,2,0:T(8,128)(2,1)} reshape(bf16[4,2,47,4096]{3,1,2,0:T(2,128)(2,1)} %param.8) | data formatting | bytes 6160384 | tf_op jit(solution)/shard_map/reshape | solution.py:411
  8.1 2.5 %copy.15.int_ref = bf16[4,2,47,32,128]{4,3,2,1,0:T(8,128)(2,1)S(1)} copy(bf16[4,2,47,32,128]{4,3,1,2,0:T(8,128)(2,1)} %reshape.16) | data formatting | bytes 6160384 | tf_op jit(solution)/shard_map/reshape | solution.py:411
  10.6 0.0 copy-start.5
  10.6 0.0 copy-start.1
  10.6 0.0 copy-start.2
  10.6 0.0 copy-start.4
  10.7 3.3 %reshape.13 = bf16[4,2,12,32,128]{4,3,1,2,0:T(8,128)(2,1)} reshape(bf16[4,2,12,4096]{3,1,2,0:T(2,128)(2,1)} %param.7) | data formatting | bytes 1572864 | tf_op jit(solution)/shard_map/reshape | solution.py:410
  13.9 0.0 copy-start.3
  13.9 2.1 %copy.13.amp_ref = bf16[4,2,12,32,128]{4,3,2,1,0:T(8,128)(2,1)} copy(bf16[4,2,12,32,128]{4,3,1,2,0:T(8,128)(2,1)} %reshape.13) | data formatting | bytes 1572864 | tf_op jit(solution)/shard_map/reshape | solution.py:410
  16.1 0.0 copy-done.5
  16.1 0.1 copy.11
  16.2 0.1 reshape.12.list_ref
  16.3 0.0 copy-done.1
  16.3 0.0 copy-done.2
  16.4 0.0 copy-done.4
  16.4 0.0 copy-start
  16.4 1.1 copy-done
  17.5 126.6 %exchange.1 = (bf16[2,6,2,1,128,128]{5,4,3,2,1,0:T(8,128)(2,1)S(1)}, bf16[2,6,2,1,128,128]{5,4,3,2,1,0:T(8,128)(2,1)S(1)}, s32[3,12]{1,0:T(4,128)S(1)}) custom-call(s32[192]{0:T(256)S(1)} %reshape.12.list_ref, s32[8]{0:T(128)S(1)} %copy-done.4, bf16[4,2,12,32,128]{4,3,2,1,0:T(8,128)(2,1)S(1)} %copy-done, bf16[4,2,47,32,128]{4,3,2,1,0:T(8,128)(2,1)S(1)} %copy.15.int_ref, ...), custom_call_target="tpu_custom_call" | custom-call | tf_op jit(solution)/shard_map/exchange/pallas_call | solution.py:413
  144.1 0.0 copy-done.3
  144.2 1.3 finish.1
  145.5 0.1 copy.14
  145.6 2.0 %reshape.15 = f32[4,2,12,4096]{3,1,2,0:T(2,128)} reshape(f32[4,2,12,32,128]{4,3,1,2,0:T(8,128)S(1)} %copy.14) | data formatting | bytes 3145728 | tf_op jit(solution)/shard_map/reshape | solution.py:455
Async XLA Ops:
  10.6 5.5 %copy-start.5 = (s32[8,12,2]{1,2,0:T(2,128)S(1)}, s32[8,12,2]{1,2,0:T(2,128)}, u32[]{:S(2)}) copy-start(s32[8,12,2]{1,2,0:T(2,128)} %param.9) | copy-start | bytes 2308
  10.6 5.7 %copy-start.1 = (bf16[256,256]{1,0:T(8,128)(2,1)S(1)}, bf16[256,256]{1,0:T(8,128)(2,1)}, u32[]{:S(2)}) copy-start(bf16[256,256]{1,0:T(8,128)(2,1)} %constant.6.clone.amat_ref) | copy-start | bytes 393220
  10.6 5.7 %copy-start.2 = (bf16[256,256]{1,0:T(8,128)(2,1)S(1)}, bf16[256,256]{1,0:T(8,128)(2,1)}, u32[]{:S(2)}) copy-start(bf16[256,256]{1,0:T(8,128)(2,1)} %constant.7.clone.wmat_ref) | copy-start | bytes 393220
  10.6 5.7 %copy-start.4 = (s32[8]{0:T(128)S(1)}, s32[8]{0:T(128)}, u32[]{:S(2)}) copy-start(s32[8]{0:T(128)} %count_ref.1) | copy-start | bytes 100
  13.9 130.2 %copy-start.3 = (bf16[128,128]{1,0:T(8,128)(2,1)S(1)}, bf16[128,128]{1,0:T(8,128)(2,1)}, u32[]{:S(2)}) copy-start(bf16[128,128]{1,0:T(8,128)(2,1)} %constant.8.clone.mat_ref) | copy-start | bytes 98308
  16.4 1.1 copy-start

commit v4 on v3

--- a/solution.py
+++ b/solution.py
@@ -48,12 +48,12 @@
 
 def exchange(
     list_ref, count_ref, amp_ref, int_ref, amat_ref, wmat_ref, own_ref, mir_ref, at_ref,
-    a_out, w_out, abuf, wbuf, cbuf, mbuf,
+    a_out, w_out, abuf, wbuf, cbuf, mbuf, wide,
     y_send, y_recv, x_send, v_send, v_recv, p_send, p_recv, keep, m_send, m_recv, n_send, n_recv,
 ):
     phases, _, span = a_out.shape[:3]
     occ = amp_ref.shape[0]
-    slots = amp_ref.shape[2]
+    slots = amp_ref.shape[1]
     half = slots // 2
     row = lax.axis_index("row")
     col = lax.axis_index("col")
@@ -140,8 +140,9 @@
 
     def pack_a():
         for i in range(occ):
-            left = amp_ref[i, 0].reshape(slots * HALF, LANES)
-            right = amp_ref[i, 1].reshape(slots * HALF, LANES)
+            wide[...] = amp_ref[i].reshape(slots * TILE, LANES).astype(jnp.float32)
+            left = wide[pl.ds(0, slots * HALF, stride=2), :].astype(jnp.bfloat16)
+            right = wide[pl.ds(1, slots * HALF, stride=2), :].astype(jnp.bfloat16)
             both = jnp.concatenate([left, right], axis=1)
             made = jnp.dot(both, amat_ref[...], preferred_element_type=jnp.float32).astype(jnp.bfloat16)
             for s in range(slots):
@@ -157,8 +158,10 @@
             for e in range(2):
                 for u in range(span):
                     tile = list_ref[(r * slots + e * half + p * span + u) * 2 + 1]
-                    left = int_ref[:, 0, tile].reshape(occ * HALF, LANES)
-                    right = int_ref[:, 1, tile].reshape(occ * HALF, LANES)
+                    at = (e * span + u) * occ * TILE
+                    wide[pl.ds(at, occ * TILE), :] = int_ref[:, tile].reshape(occ * TILE, LANES).astype(jnp.float32)
+                    left = wide[pl.ds(at, occ * HALF, stride=2), :].astype(jnp.bfloat16)
+                    right = wide[pl.ds(at + 1, occ * HALF, stride=2), :].astype(jnp.bfloat16)
                     both = jnp.concatenate([left, right], axis=1)
                     made = jnp.dot(both, wmat_ref[...], preferred_element_type=jnp.float32).astype(jnp.bfloat16)
                     for k in range(occ):
@@ -360,7 +363,7 @@
 
 
 def finish(at_ref, own_ref, mir_ref, mat_ref, out_ref, turn):
-    slots = out_ref.shape[2]
+    slots = out_ref.shape[1]
     half = slots // 2
     span = own_ref.shape[3]
     lane = lax.broadcasted_iota(jnp.int32, (HALF, LANES), 1)
@@ -389,8 +392,8 @@
                 top = mine[u * TILE : u * TILE + HALF]
                 bottom = mine[u * TILE + HALF : (u + 1) * TILE]
                 first, second = fold((top + even) * live, (bottom + odd) * live)
-                out_ref[i, 0, s] = first
-                out_ref[i, 1, s] = second
+                out_ref[i, s, pl.ds(0, HALF, stride=2), :] = first
+                out_ref[i, s, pl.ds(1, HALF, stride=2), :] = second
 
 
 def on_device(amplitudes, integrals, pair_lists, tile_counts):
@@ -407,8 +410,10 @@
     dma = pltpu.SemaphoreType.DMA
 
     lists = pair_lists.reshape(-1)
-    amp = amplitudes.reshape(occ_row, occ_col, slots, HALF, LANES)
-    integ = integrals.reshape(occ_row, occ_col, tiles, HALF, LANES)
+    amp = amplitudes.reshape(occ_row, occ_col, slots, HALF, LANES).transpose(0, 2, 3, 1, 4)
+    amp = amp.reshape(occ_row, slots, TILE, LANES)
+    integ = integrals.reshape(occ_row, occ_col, tiles, HALF, LANES).transpose(0, 2, 3, 1, 4)
+    integ = integ.reshape(occ_row, tiles, TILE, LANES)
 
     own, mirror, places = pl.pallas_call(
         exchange,
@@ -427,6 +432,7 @@
             pltpu.VMEM((PHASES, 4, 2, span, 2, block, LANES), bf16),
             pltpu.VMEM((PHASES, 2, 2, span, LANES, LANES), bf16),
             pltpu.VMEM((PHASES, 2, 2, span, LANES, LANES), bf16),
+            pltpu.VMEM((max(slots * TILE, 2 * span * block), LANES), f32),
             dma((PHASES, 5, 2)),
             dma((PHASES, 2, 4, 2)),
             dma((PHASES, 4, 2)),
@@ -446,12 +452,13 @@
     packed = pl.pallas_call(
         finish,
         name="finish",
-        out_shape=jax.ShapeDtypeStruct((occ_row, occ_col, slots, HALF, LANES), f32),
+        out_shape=jax.ShapeDtypeStruct((occ_row, slots, TILE, LANES), f32),
         in_specs=[smem, vmem, vmem, vmem],
         out_specs=vmem,
         scratch_shapes=[pltpu.VMEM((2, 2, LANES, LANES), f32)],
         compiler_params=pltpu.CompilerParams(vmem_limit_bytes=32 << 20),
     )(places, own, mirror, jnp.asarray(untangle_matrix(), bf16))
+    packed = packed.reshape(occ_row, slots, HALF, occ_col, LANES).transpose(0, 3, 1, 2, 4)
     return packed.reshape(occ_row, occ_col, slots, square)
 
 

time: 148 us -> 136 us (0.919)
  local copies, waits for them, and re-layouts: 19.5 us -> 6.44 us
    reshape x5 -> x0, local copies, waits for them, and re-layouts: 18 us -> none  [the longest x2 10.6 us: on_device(): integ = integrals.reshape(occ_row, occ_col, tiles, HALF, LANES)]
    unnamed x13, local copies, waits for them, and re-layouts: 1.29 us -> 6.3 us
where the time goes in v4:
time: 136 us
  Pallas kernels  129 us (95%)
  local copies, waits for them, and re-layouts  6.44 us (5%)
    pallas_call x1, Pallas kernels, on_device(): pl.pallas_call(exchange, name='exchange', out_shape=(jax.ShapeDtypeStruct...  127 us
    unnamed x13, local copies, waits for them, and re-layouts  6.3 us

profile of v4, /device:TPU:3, one launch (start us, length us, event | category | flops | bytes accessed | tf_op | source)
XLA Modules:
  0.0 135.8 jit_solution(17814059513676261989)
XLA Ops:
  0.0 0.0 copy-start.4
  0.0 0.8 copy.11
  0.8 0.1 reshape.21.list_ref
  1.0 0.0 copy-start
  1.0 1.9 %copy-done = bf16[4,2,47,4096]{3,1,2,0:T(2,128)(2,1)S(1)} copy-done((bf16[4,2,47,4096]{3,1,2,0:T(2,128)(2,1)S(1)}, bf16[4,2,47,4096]{3,1,2,0:T(2,128)(2,1)}, u32[]{:S(2)}) %copy-start) | copy-done | bytes 3080216
  2.9 0.0 copy-start.1
  2.9 1.1 copy-done.1
  4.0 0.0 copy-start.2
  4.0 0.9 copy-done.2
  4.9 0.0 copy-start.3
  4.9 0.9 copy-done.3
  5.8 0.0 copy-start.5
  5.8 0.7 copy-done.5
  6.5 126.8 %exchange.1 = (bf16[2,6,2,1,128,128]{5,4,3,2,1,0:T(8,128)(2,1)S(1)}, bf16[2,6,2,1,128,128]{5,4,3,2,1,0:T(8,128)(2,1)S(1)}, s32[3,12]{1,0:T(4,128)S(1)}) custom-call(s32[192]{0:T(256)S(1)} %reshape.21.list_ref, s32[8]{0:T(128)S(1)} %copy-done.5, bf16[4,12,64,128]{3,2,1,0:T(8,128)(2,1)S(1)} %bitcast.16, bf16[4,47,64,128]{3,2,1,0:T(8,128)(2,1)S(1)} %bitcast.15, ...), custom_call_target="tpu_custom_call" | custom-call | tf_op jit(solution)/shard_map/exchange/pallas_call | solution.py:418
  133.3 0.0 copy-done.4
  133.3 2.5 %finish.1 = f32[4,12,64,128]{3,2,1,0:T(8,128)} custom-call(s32[3,12]{1,0:T(4,128)S(1)} %get-tuple-element.8.at_ref, bf16[2,6,2,1,128,128]{5,4,3,2,1,0:T(8,128)(2,1)S(1)} %get-tuple-element.9.own_ref, bf16[2,6,2,1,128,128]{5,4,3,2,1,0:T(8,128)(2,1)S(1)} %get-tuple-element.10.mir_ref, bf16[128,128]{1,0:T(8,128)(2,1)S(1)} %copy-done.4), custom_call_target="tpu_custom_call" | custom-call | tf_op jit(solution)/shard_map/finish/pallas_call | solution.py:452
Async XLA Ops:
  0.0 133.3 %copy-start.4 = (bf16[128,128]{1,0:T(8,128)(2,1)S(1)}, bf16[128,128]{1,0:T(8,128)(2,1)}, u32[]{:S(2)}) copy-start(bf16[128,128]{1,0:T(8,128)(2,1)} %constant.8.clone.mat_ref) | copy-start | bytes 98308
  1.0 1.9 %copy-start = (bf16[4,2,47,4096]{3,1,2,0:T(2,128)(2,1)S(1)}, bf16[4,2,47,4096]{3,1,2,0:T(2,128)(2,1)}, u32[]{:S(2)}) copy-start(bf16[4,2,47,4096]{3,1,2,0:T(2,128)(2,1)} %param.8) | copy-start | bytes 9240580
  2.9 1.1 copy-start.1
  4.0 0.9 copy-start.2
  4.9 0.9 copy-start.3
  5.8 0.7 copy-start.5

commit v5 on v4

--- a/solution.py
+++ b/solution.py
@@ -14,8 +14,8 @@
 HALF = TILE // 2
 LANES = 128
 PHASES = 6
-A_AHEAD = 3
-W_AHEAD = 3
+A_AHEAD = 2
+W_AHEAD = 2
 LAG = 2
 RELAYS = (
     (0, 51, 48, 55, 5, 58, 3, 59, 7, 49, 38, 4, 11, 50, 6, 54, 18, 44, 43, 36, 42, 27, 20, 47, 24, 52, 28, 16, 46, 40, 22, 45, 23, 35, 17, 41, 34, 39, 25, 19, 29, 37, 21, 32, 31, 2, 30, 33, 13, 61, 12, 62, 9, 26, 14, 53, 8, 60, 1, 57, 10, 56, 15, 63),
@@ -28,13 +28,12 @@
 
 
 def merge_matrix(permute):
-    out = np.zeros((2 * LANES, 2 * LANES), np.float32)
-    for operand in range(2):
-        for h in range(2):
-            for c in range(TILE):
-                place = (c % 2) * HALF + c // 2 if permute else c
-                out[operand * LANES + h * TILE + c, h * LANES + operand * TILE + place] = 1.0
-    return out
+    row = lax.broadcasted_iota(jnp.int32, (2 * LANES, 2 * LANES), 0)
+    col = lax.broadcasted_iota(jnp.int32, (2 * LANES, 2 * LANES), 1)
+    c = row & (TILE - 1)
+    place = (c & 1) * HALF + (c >> 1) if permute else c
+    target = ((row >> 6) & 1) * LANES + (row >> 7) * TILE + place
+    return jnp.where(col == target, 1.0, 0.0).astype(jnp.bfloat16)
 
 
 def untangle_matrix():
@@ -47,11 +46,15 @@
 
 
 def exchange(
-    list_ref, count_ref, amp_ref, int_ref, amat_ref, wmat_ref, own_ref, mir_ref, at_ref,
-    a_out, w_out, abuf, wbuf, cbuf, mbuf, wide,
+    list_ref, count_ref, amp_any, int_any, own_ref, mir_ref, at_ref,
+    amp_ref, int_ref, amat_ref, wmat_ref, a_out, w_out, abuf, wbuf, cbuf, mbuf, wide, load,
     y_send, y_recv, x_send, v_send, v_recv, p_send, p_recv, keep, m_send, m_recv, n_send, n_recv,
 ):
     phases, _, span = a_out.shape[:3]
+    amp_load = pltpu.make_async_copy(amp_any, amp_ref, load.at[0])
+    int_load = pltpu.make_async_copy(int_any, int_ref, load.at[1])
+    amp_load.start()
+    int_load.start()
     occ = amp_ref.shape[0]
     slots = amp_ref.shape[1]
     half = slots // 2
@@ -124,7 +127,6 @@
 
         total = total + jnp.where(goes[n] != here, 1, 0) + jnp.where(ends[n] != here, 2, 0)
 
-    pl.semaphore_wait(barrier, total)
 
     def remote(src, dst, send, recv, place):
         return pltpu.make_async_remote_copy(
@@ -157,7 +159,7 @@
             xi, zd = r // 4, lax.rem(r, 4)
             for e in range(2):
                 for u in range(span):
-                    tile = list_ref[(r * slots + e * half + p * span + u) * 2 + 1]
+                    tile = list_ref[r, 1, e * half + p * span + u]
                     at = (e * span + u) * occ * TILE
                     wide[pl.ds(at, occ * TILE), :] = int_ref[:, tile].reshape(occ * TILE, LANES).astype(jnp.float32)
                     left = wide[pl.ds(at, occ * HALF, stride=2), :].astype(jnp.bfloat16)
@@ -326,22 +328,31 @@
 
     def find():
         for s in range(slots):
-            a = list_ref[(row * slots + s) * 2]
-            b = list_ref[(row * slots + s) * 2 + 1]
+            a = list_ref[row, 0, s]
+            b = list_ref[row, 1, s]
             found = jnp.int32(-1)
             for t in range(slots):
-                same = (list_ref[(chip * slots + t) * 2] == b) & (list_ref[(chip * slots + t) * 2 + 1] == a)
+                same = (list_ref[chip, 0, t] == b) & (list_ref[chip, 1, t] == a)
                 found = jnp.where(same & (t < count_ref[chip]), t, found)
             at_ref[0, s] = jnp.maximum(found, 0)
             at_ref[1, s] = (found >= 0).astype(jnp.int32)
             at_ref[2, s] = (s < count_ref[row]).astype(jnp.int32)
 
+    amat_ref[...] = merge_matrix(True)
+    wmat_ref[...] = merge_matrix(False)
+    amp_load.wait()
     pack_a()
-    for p in range(min(A_AHEAD, phases)):
+    int_load.wait()
+    pack_w(0)
+    pl.semaphore_wait(barrier, total)
+    send_y(0)
+    send_v(0)
+    for p in range(1, min(A_AHEAD, phases)):
         send_y(p)
     for p in range(min(W_AHEAD, phases)):
-        pack_w(p)
-        send_v(p)
+        if p > 0:
+            pack_w(p)
+            send_v(p)
         if p == 0:
             pass_on(0)
     find()
@@ -407,9 +418,10 @@
     vmem = pl.BlockSpec(memory_space=pltpu.VMEM)
     smem = pl.BlockSpec(memory_space=pltpu.SMEM)
     anywhere = pl.BlockSpec(memory_space=pl.ANY)
+    hbm = pl.BlockSpec(memory_space=pltpu.MemorySpace.HBM)
     dma = pltpu.SemaphoreType.DMA
 
-    lists = pair_lists.reshape(-1)
+    lists = pair_lists.transpose(0, 2, 1)
     amp = amplitudes.reshape(occ_row, occ_col, slots, HALF, LANES).transpose(0, 2, 3, 1, 4)
     amp = amp.reshape(occ_row, slots, TILE, LANES)
     integ = integrals.reshape(occ_row, occ_col, tiles, HALF, LANES).transpose(0, 2, 3, 1, 4)
@@ -423,9 +435,13 @@
             jax.ShapeDtypeStruct((2, PHASES, 2, span, LANES, LANES), bf16),
             jax.ShapeDtypeStruct((3, slots), jnp.int32),
         ),
-        in_specs=[smem, smem, vmem, vmem, vmem, vmem],
+        in_specs=[smem, smem, hbm, hbm],
         out_specs=(anywhere, anywhere, smem),
         scratch_shapes=[
+            pltpu.VMEM((occ_row, slots, TILE, LANES), bf16),
+            pltpu.VMEM((occ_row, tiles, TILE, LANES), bf16),
+            pltpu.VMEM((2 * LANES, 2 * LANES), bf16),
+            pltpu.VMEM((2 * LANES, 2 * LANES), bf16),
             pltpu.VMEM((PHASES, 2, span, block, LANES), bf16),
             pltpu.VMEM((PHASES, 4, 2, span, 2, block, LANES), bf16),
             pltpu.VMEM((PHASES, 2, 4, 2, span, block, LANES), bf16),
@@ -433,6 +449,7 @@
             pltpu.VMEM((PHASES, 2, 2, span, LANES, LANES), bf16),
             pltpu.VMEM((PHASES, 2, 2, span, LANES, LANES), bf16),
             pltpu.VMEM((max(slots * TILE, 2 * span * block), LANES), f32),
+            dma((2,)),
             dma((PHASES, 5, 2)),
             dma((PHASES, 2, 4, 2)),
             dma((PHASES, 4, 2)),
@@ -446,8 +463,8 @@
             dma((PHASES, 2)),
             dma((PHASES, 2)),
         ],
-        compiler_params=pltpu.CompilerParams(collective_id=0, has_side_effects=True, vmem_limit_bytes=48 << 20),
-    )(lists, tile_counts, amp, integ, jnp.asarray(merge_matrix(True), bf16), jnp.asarray(merge_matrix(False), bf16))
+        compiler_params=pltpu.CompilerParams(collective_id=0, has_side_effects=True, vmem_limit_bytes=62 << 20),
+    )(lists, tile_counts, amp, integ)
 
     packed = pl.pallas_call(
         finish,

time: 136 us -> 133 us (0.978)
  local copies, waits for them, and re-layouts: 6.44 us -> 2.94 us
    unnamed x13 -> x8, local copies, waits for them, and re-layouts: 6.3 us -> 2.94 us
where the time goes in v5:
time: 133 us; the launch traced here: 132 us
  Pallas kernels  129 us (97%)
  local copies, waits for them, and re-layouts  2.94 us (2%)
    pallas_call x1, Pallas kernels, on_device(): pl.pallas_call(exchange, name='exchange', out_shape=(jax.ShapeDtypeStruct...  127 us
    unnamed x8, local copies, waits for them, and re-layouts  2.94 us

profile of v5, /device:TPU:3, one launch (start us, length us, event | category | flops | bytes accessed | tf_op | source)
XLA Modules:
  0.0 132.3 jit_solution(2263690259928318787)
XLA Ops:
  0.0 0.0 copy-start.2
  0.0 126.9 %exchange.1 = (bf16[2,6,2,1,128,128]{5,4,3,2,1,0:T(8,128)(2,1)}, bf16[2,6,2,1,128,128]{5,4,3,2,1,0:T(8,128)(2,1)}, s32[3,12]{1,0:T(4,128)}) custom-call(s32[8,2,12]{2,1,0:T(2,128)} %bitcast.18, s32[8]{0:T(128)} %count_ref.1, bf16[4,12,64,128]{3,2,1,0:T(8,128)(2,1)} %bitcast.17, bf16[4,47,64,128]{3,2,1,0:T(8,128)(2,1)} %bitcast.16), custom_call_target="tpu_custom_call" | custom-call | tf_op jit(solution)/shard_map/exchange/pallas_call | solution.py:430
  126.9 0.0 copy-done.2
  126.9 0.0 copy-start
  127.0 1.1 copy-done
  128.1 0.0 copy-start.1
  128.1 1.1 copy-done.1
  129.2 0.0 copy-start.3
  129.2 0.7 copy-done.3
  129.9 2.4 %finish.1 = f32[4,12,64,128]{3,2,1,0:T(8,128)} custom-call(s32[3,12]{1,0:T(4,128)S(1)} %copy-done.3, bf16[2,6,2,1,128,128]{5,4,3,2,1,0:T(8,128)(2,1)S(1)} %copy-done, bf16[2,6,2,1,128,128]{5,4,3,2,1,0:T(8,128)(2,1)S(1)} %copy-done.1, bf16[128,128]{1,0:T(8,128)(2,1)S(1)} %copy-done.2), custom_call_target="tpu_custom_call" | custom-call | tf_op jit(solution)/shard_map/finish/pallas_call | solution.py:469
Async XLA Ops:
  0.0 126.9 %copy-start.2 = (bf16[128,128]{1,0:T(8,128)(2,1)S(1)}, bf16[128,128]{1,0:T(8,128)(2,1)}, u32[]{:S(2)}) copy-start(bf16[128,128]{1,0:T(8,128)(2,1)} %constant.2.clone.mat_ref) | copy-start | bytes 98308
  126.9 1.1 copy-start
  128.1 1.1 copy-start.1
  129.2 0.7 copy-start.3

commit v6 on v5

--- a/solution.py
+++ b/solution.py
@@ -2,7 +2,6 @@
 
 import jax
 import jax.numpy as jnp
-import numpy as np
 from jax import lax
 from jax.experimental import pallas as pl
 from jax.experimental.pallas import tpu as pltpu
@@ -18,12 +17,9 @@
 W_AHEAD = 2
 LAG = 2
 RELAYS = (
-    (0, 51, 48, 55, 5, 58, 3, 59, 7, 49, 38, 4, 11, 50, 6, 54, 18, 44, 43, 36, 42, 27, 20, 47, 24, 52, 28, 16, 46, 40, 22, 45, 23, 35, 17, 41, 34, 39, 25, 19, 29, 37, 21, 32, 31, 2, 30, 33, 13, 61, 12, 62, 9, 26, 14, 53, 8, 60, 1, 57, 10, 56, 15, 63),
-    (3, 0, 5, 2, 50, 62, 53, 54, 8, 60, 48, 59, 1, 63, 6, 57, 32, 41, 44, 28, 42, 22, 29, 34, 40, 43, 16, 58, 31, 47, 46, 23, 17, 26, 38, 24, 45, 35, 7, 20, 33, 21, 25, 37, 19, 36, 18, 39, 4, 9, 14, 30, 11, 56, 15, 51, 10, 61, 49, 13, 27, 55, 12, 52),
-    (14, 56, 0, 53, 62, 9, 10, 49, 59, 48, 5, 8, 3, 7, 54, 51, 21, 46, 44, 36, 57, 42, 30, 27, 20, 40, 43, 28, 17, 24, 39, 19, 29, 33, 23, 37, 16, 35, 22, 32, 25, 45, 34, 38, 18, 31, 47, 41, 26, 12, 2, 60, 6, 63, 4, 55, 13, 58, 61, 1, 52, 50, 15, 11),
-    (1, 45, 8, 63, 60, 6, 53, 37, 52, 51, 4, 48, 2, 14, 49, 54, 24, 20, 19, 46, 31, 29, 35, 44, 27, 18, 58, 30, 26, 41, 25, 42, 22, 32, 10, 40, 47, 21, 38, 39, 17, 33, 16, 36, 28, 34, 23, 43, 9, 50, 61, 57, 56, 5, 12, 15, 7, 59, 62, 0, 11, 55, 13, 3),
-    (8, 48, 5, 52, 6, 15, 54, 58, 4, 57, 3, 53, 14, 34, 39, 51, 63, 43, 21, 47, 25, 30, 26, 61, 37, 36, 44, 29, 40, 46, 19, 50, 17, 18, 41, 33, 27, 16, 20, 22, 45, 42, 28, 23, 35, 32, 24, 38, 2, 9, 13, 49, 56, 7, 10, 12, 31, 1, 0, 60, 55, 59, 62, 11),
-    (0, 48, 4, 54, 15, 59, 7, 51, 58, 56, 3, 52, 2, 62, 57, 10, 28, 43, 24, 47, 30, 41, 27, 42, 29, 33, 18, 31, 26, 25, 34, 46, 16, 17, 20, 38, 35, 45, 40, 23, 32, 39, 37, 21, 22, 19, 36, 44, 49, 8, 1, 13, 55, 11, 63, 50, 5, 53, 9, 61, 14, 6, 60, 12),
+    (63, 48, 55, 56, 51, 54, 2, 7, 8, 0, 35, 52, 49, 50, 4, 10, 43, 33, 44, 41, 26, 45, 31, 18, 21, 24, 16, 40, 29, 42, 20, 46, 17, 32, 30, 39, 19, 27, 6, 28, 34, 36, 25, 38, 23, 47, 37, 5, 62, 60, 53, 61, 9, 14, 3, 15, 57, 58, 1, 13, 22, 11, 12, 59),
+    (12, 5, 41, 55, 54, 50, 7, 10, 3, 58, 52, 60, 2, 62, 39, 48, 28, 40, 21, 47, 42, 22, 37, 46, 24, 44, 31, 19, 26, 34, 43, 30, 29, 45, 36, 25, 20, 16, 27, 38, 32, 6, 33, 17, 18, 1, 23, 35, 4, 57, 0, 14, 8, 51, 61, 63, 56, 53, 13, 9, 11, 59, 15, 49),
+    (48, 0, 56, 36, 14, 3, 10, 2, 61, 51, 5, 4, 54, 55, 6, 50, 24, 42, 47, 44, 25, 26, 34, 40, 31, 29, 28, 32, 30, 22, 46, 45, 16, 17, 1, 20, 18, 35, 23, 37, 21, 33, 38, 41, 19, 43, 27, 39, 11, 53, 13, 49, 7, 52, 8, 59, 9, 57, 62, 12, 60, 63, 58, 15),
 )
 
 
@@ -37,12 +33,10 @@
 
 
 def untangle_matrix():
-    out = np.zeros((LANES, LANES), np.float32)
-    for j in range(2):
-        for h in range(2):
-            for p in range(HALF):
-                out[j * TILE + h * HALF + p, j * TILE + 2 * p + h] = 1.0
-    return out
+    row = lax.broadcasted_iota(jnp.int32, (LANES, LANES), 0)
+    col = lax.broadcasted_iota(jnp.int32, (LANES, LANES), 1)
+    target = (row & TILE) + (row & (HALF - 1)) * 2 + ((row >> 5) & 1)
+    return jnp.where(col == target, 1.0, 0.0).astype(jnp.bfloat16)
 
 
 def exchange(
@@ -373,7 +367,11 @@
         close(p)
 
 
-def finish(at_ref, own_ref, mir_ref, mat_ref, out_ref, turn):
+def finish(at_ref, own_any, mir_any, out_ref, own_ref, mir_ref, turn, load):
+    copies = [pltpu.make_async_copy(own_any, own_ref, load.at[0]), pltpu.make_async_copy(mir_any, mir_ref, load.at[1])]
+    for copy in copies:
+        copy.start()
+    matrix = untangle_matrix()
     slots = out_ref.shape[1]
     half = slots // 2
     span = own_ref.shape[3]
@@ -385,6 +383,8 @@
         second = jnp.where(low, pltpu.roll(even, TILE, 1), odd)
         return first, second
 
+    for copy in copies:
+        copy.wait()
     for s in range(slots):
         t = at_ref[0, s]
         hit = at_ref[1, s].astype(jnp.float32)
@@ -393,7 +393,7 @@
         se, sp, su = s // half, s % half // span, s % span
         for jp in range(2):
             block = mir_ref[te, tp, jp, tu]
-            turned = lax.dot_general(block, mat_ref[...], (((0,), (0,)), ((), ())), preferred_element_type=jnp.float32)
+            turned = lax.dot_general(block, matrix, (((0,), (0,)), ((), ())), preferred_element_type=jnp.float32)
             turn[s % 2, jp] = turned * hit
             mine = own_ref[se, sp, jp, su].astype(jnp.float32)
             for u in range(2):
@@ -470,11 +470,16 @@
         finish,
         name="finish",
         out_shape=jax.ShapeDtypeStruct((occ_row, slots, TILE, LANES), f32),
-        in_specs=[smem, vmem, vmem, vmem],
+        in_specs=[smem, hbm, hbm],
         out_specs=vmem,
-        scratch_shapes=[pltpu.VMEM((2, 2, LANES, LANES), f32)],
-        compiler_params=pltpu.CompilerParams(vmem_limit_bytes=32 << 20),
-    )(places, own, mirror, jnp.asarray(untangle_matrix(), bf16))
+        scratch_shapes=[
+            pltpu.VMEM(own.shape, bf16),
+            pltpu.VMEM(mirror.shape, bf16),
+            pltpu.VMEM((2, 2, LANES, LANES), f32),
+            dma((2,)),
+        ],
+        compiler_params=pltpu.CompilerParams(vmem_limit_bytes=62 << 20),
+    )(places, own, mirror)
     packed = packed.reshape(occ_row, slots, HALF, occ_col, LANES).transpose(0, 3, 1, 2, 4)
     return packed.reshape(occ_row, occ_col, slots, square)
 

time: 133 us -> 129 us (0.970)
  the two profiles are of different devices: /device:TPU:3 before, /device:TPU:71 now
where the time goes in v6:
time: 129 us
  Pallas kernels  129 us (100%)
    pallas_call x1, Pallas kernels, on_device(): pl.pallas_call(exchange, name='exchange', out_shape=(jax.ShapeDtypeStruct...  125 us
    pallas_call x1, Pallas kernels, on_device(): pl.pallas_call(finish, name='finish', out_shape=jax.ShapeDtypeStruct((occ...  3.98 us

profile of v6, /device:TPU:71, one launch (start us, length us, event | category | flops | bytes accessed | tf_op | source)
XLA Modules:
  0.0 128.7 jit_solution(10377332800808620376)
XLA Ops:
  0.0 124.8 %exchange.1 = (bf16[2,6,2,1,128,128]{5,4,3,2,1,0:T(8,128)(2,1)}, bf16[2,6,2,1,128,128]{5,4,3,2,1,0:T(8,128)(2,1)}, s32[3,12]{1,0:T(4,128)}) custom-call(s32[8,2,12]{2,1,0:T(2,128)} %bitcast.18, s32[8]{0:T(128)} %count_ref.1, bf16[4,12,64,128]{3,2,1,0:T(8,128)(2,1)} %bitcast.17, bf16[4,47,64,128]{3,2,1,0:T(8,128)(2,1)} %bitcast.16), custom_call_target="tpu_custom_call" | custom-call | tf_op jit(solution)/shard_map/exchange/pallas_call | solution.py:430
  124.8 4.0 %finish.1 = f32[4,12,64,128]{3,2,1,0:T(8,128)} custom-call(s32[3,12]{1,0:T(4,128)} %get-tuple-element.8.at_ref, bf16[2,6,2,1,128,128]{5,4,3,2,1,0:T(8,128)(2,1)} %get-tuple-element.9.own_any, bf16[2,6,2,1,128,128]{5,4,3,2,1,0:T(8,128)(2,1)} %get-tuple-element.10.mir_any), custom_call_target="tpu_custom_call" | custom-call | tf_op jit(solution)/shard_map/finish/pallas_call | solution.py:469
